TPU v7x, 256 devices: a whole 4x4x8 slice. The times are simulated.
256 devices in a mesh: expert: 8 (over y, core), tensor: 8 (over z), dp: 4 (over x).
Axes of the slice: x: 4, y: 4, z: 8, core: 2. Of those that a mesh axis runs over, the one named last changes fastest.
Arguments:
- tokens: bfloat16 [4096, 4096], P(('expert', 'dp'), 'tensor'), may hold values from -9 to 9
- expert_ids: int32 [4096, 2], P(('expert', 'dp')), may hold values from 0 to 7, all different within a row; in each aligned block of 128 rows (0 to 127, 128 to 255, ...) at most 40 rows name the same one
- gate_fixed: int32 [4096, 2], P(('expert', 'dp')), may hold values from 1 to 65536
- w_gate: bfloat16 [8, 4096, 14336], P('expert', None, ('tensor', 'dp')), may hold values from -0.09375 to 0.09375
- w_up: bfloat16 [8, 4096, 14336], P('expert', None, ('tensor', 'dp')), may hold values from -0.09375 to 0.09375
- w_down: bfloat16 [8, 14336, 4096], P('expert', ('tensor', 'dp')), may hold values from -1 to 1, as said below
- down_check: bfloat16 [8, 14336], P('expert', ('tensor', 'dp')), may hold values from -4 to 4, as said below
Outputs:
- expert_mix: float32 [4096, 4096], P(('expert', 'dp'), 'tensor')
- check_residual: float32 [4096], P(('expert', 'dp'))
- alarm_level: float32 [], replicated
Inputs may be any that keep to these rules, and one draw needn't show every extreme that they name: `expert_ids`: each token names 2 different experts; among the rows of one device (aligned blocks of 128 rows) no expert is named more than 40 times, a bound that some block reaches. `w_down`: weights of order 14336 ** -0.5. down_check[x, f] is the sum over the 4096 features of w_down[x, f, :], except on some hidden units where it is corrupted.
All inputs are finite; a program needn't handle non-finite values.
Results may differ from a plain program's by a relative error of at most 0.015.
Values may be sent and summed in bfloat16 or wider, within the bound.
A program may use at most 128 MiB of HBM per device.

v0:
```python
import math

import jax
import jax.numpy as jnp
from jax import lax
from jax.sharding import PartitionSpec as P

D = 4096
CAP = 40


def scatter_axes(x, axes, dim):
    if not axes:
        return x
    nearer = lax.psum_scatter(x, axes[0], scatter_dimension=dim, tiled=True)
    return scatter_axes(nearer, axes[1:], dim)


def copy_for_each(x, axis):
    copies = jnp.broadcast_to(x, (lax.axis_size(axis), *x.shape))
    return lax.all_to_all(copies, axis, split_axis=0, concat_axis=0, tiled=True)


def taken_together(x, axis):
    return copy_for_each(x, axis).sum(axis=0)


def in_one_piece(arrays, axis, split_dim, concat_dim, along):
    columns = [a.reshape(*a.shape[:along], -1) for a in arrays]
    both = jnp.concatenate(columns, axis=along)
    filled, at, outs = (
        lax.all_to_all(both, axis, split_axis=split_dim, concat_axis=concat_dim, tiled=True),
        0,
        [],
    )
    for a, column in zip(arrays, columns):
        share = filled[..., at : at + column.shape[along]]
        outs.append(share.reshape(*share.shape[:along], *a.shape[along:]))
        at += column.shape[along]
    return tuple(outs)


def body(tokens, expert_ids, gate_fixed, w_gate, w_up, w_down, down_check):
    groups = lax.axis_size("expert")
    stripes = lax.axis_size("tensor")
    replica_count = lax.axis_size("dp")
    local_experts = w_gate.shape[0]
    experts = groups * local_experts
    row_count = tokens.shape[0]
    columns = tokens.shape[1]
    flat_ids = expert_ids.reshape(-1)
    onehot = (flat_ids[:, None] == jnp.arange(experts, dtype=jnp.int32)[None, :]).astype(jnp.int32)
    before = jnp.cumsum(onehot, axis=0) - onehot
    position = jnp.sum(before * onehot, axis=1)
    slots = flat_ids * CAP + position
    repeated = jnp.repeat(tokens, 2, axis=0)
    send_buffer = jnp.zeros((experts * CAP, columns), jnp.bfloat16).at[slots].set(repeated)
    send_buffer = send_buffer.reshape(groups, local_experts, CAP, columns)
    received = lax.all_to_all(send_buffer, "expert", split_axis=0, concat_axis=0, tiled=True)
    grouped = lax.all_gather(received[None], ("tensor", "dp"), axis=0, tiled=True)
    grouped = grouped.reshape(stripes, replica_count, groups, local_experts, CAP, columns)
    block_rows = grouped[:, :, :, 0].reshape(stripes, -1, columns)
    gate_weights = w_gate[0].reshape(stripes, columns, -1)
    up_weights = w_up[0].reshape(stripes, columns, -1)
    gate_act = jnp.einsum(
        "trc,tcf->rf", block_rows, gate_weights, preferred_element_type=jnp.float32
    )
    up_act = jnp.einsum("trc,tcf->rf", block_rows, up_weights, preferred_element_type=jnp.float32)
    hidden = (jax.nn.silu(gate_act) * up_act).astype(jnp.bfloat16)
    down_weights = w_down[0].reshape(-1, stripes, columns)
    partial_value = jnp.einsum(
        "rf,ftc->trc", hidden, down_weights, preferred_element_type=jnp.float32
    )
    outputs = [partial_value.reshape(stripes, replica_count, groups, CAP, columns)]
    check_val = jnp.dot(hidden, down_check[0], preferred_element_type=jnp.float32)
    checks = [check_val.reshape(replica_count, groups, CAP)]
    partial_terms = jnp.stack(outputs, axis=3).reshape(-1, columns)
    expert_out = scatter_axes(partial_terms.astype(jnp.bfloat16), ("tensor", "dp"), 0).astype(
        jnp.float32
    )
    expert_out = expert_out.reshape(groups, local_experts, CAP, columns)
    check_all = taken_together(jnp.stack(checks, axis=2), ("tensor", "dp"))
    own_checks = lax.dynamic_index_in_dim(check_all, lax.axis_index("dp"), 0, keepdims=False)
    returned, returned_chk = tuple(
        (
            part.astype(jnp.float32)
            for part in in_one_piece(
                (expert_out.astype(jnp.bfloat16), own_checks.astype(jnp.bfloat16)),
                "expert",
                0,
                0,
                3,
            )
        )
    )
    picked = returned.reshape(experts * CAP, columns)[slots].reshape(row_count, 2, columns)
    picked_chk = returned_chk.reshape(-1)[slots].reshape(row_count, 2)
    weights = gate_fixed.astype(jnp.float32)
    weights = weights / jnp.sum(weights, axis=1, keepdims=True)
    combined = jnp.sum(picked * weights[:, :, None], axis=1)
    row_total = taken_together(jnp.sum(combined, axis=1), "tensor")
    check_residual = (row_total - jnp.sum(weights * picked_chk, axis=1)) / math.sqrt(D)
    scores = jnp.sum(check_residual * check_residual)
    alarm_level = taken_together(scores, ("expert", "dp")) / (row_count * groups * replica_count)
    return (combined, check_residual, alarm_level)


def solution(mesh):
    return jax.shard_map(
        body,
        mesh=mesh,
        in_specs=(
            P(("expert", "dp"), "tensor"),
            P(("expert", "dp"), None),
            P(("expert", "dp"), None),
            P("expert", None, ("tensor", "dp")),
            P("expert", None, ("tensor", "dp")),
            P("expert", ("tensor", "dp"), None),
            P("expert", ("tensor", "dp")),
        ),
        out_specs=(P(("expert", "dp"), "tensor"), P(("expert", "dp")), P()),
        check_vma=False,
    )
```

profile of v0, /device:TPU:1, one launch (start us, length us, event | category | flops | bytes accessed | tf_op | source)
XLA Modules:
  0.0 359.9 jit_solution(17914635239671109024)
XLA Ops:
  7.2 0.0 all-gather.3.cloned.1.call-start
  7.2 0.8 copy.54
  8.0 0.1 eq.29
  8.2 0.1 eq.25
  8.3 0.7 broadcast_multiply_fusion
  9.0 0.6 reduce-window.6
  9.6 0.2 slice_reduce_fusion
  9.8 0.1 copy.53
  9.9 0.1 mul.49
  10.1 1.0 broadcast_in_dim.25
  11.1 0.1 reshape.160
  11.2 0.1 fusion.21
  11.3 1.6 scatter_custom_fusion
  12.9 13.7 %all_to_all.27 = bf16[8,1,40,512]{3,2,1,0:T(8,128)(2,1)} all-to-all(bf16[8,1,40,512]{3,2,1,0:T(8,128)(2,1)S(1)} %bitcast.71), channel_id=1, replica_groups=mesh['expert'=8,'tensor'=8,'dp'=4] {'expert'}, dimensions={0} | all-to-all | bytes 655360 | tf_op jit(solution)/shard_map/all_to_all | solution.py:59
  26.7 0.0 all-gather.3.cloned.1.call-update
  26.7 0.2 reduce-scatter.3.cloned.1.call-start
  26.9 5.9 %copy.68 = bf16[56,8,8,512]{3,2,1,0:T(8,128)(2,1)} copy(bf16[56,8,8,512]{3,1,2,0:T(8,128)(2,1)} %bitcast.65) | data formatting | bytes 7340032
  32.9 3.8 %copy.69 = bf16[56,8,8,512]{3,2,1,0:T(8,128)(2,1)} copy(bf16[56,8,8,512]{3,1,2,0:T(8,128)(2,1)S(1)} %bitcast.66) | data formatting | bytes 7340032
  36.7 3.9 %copy.70 = bf16[56,8,8,512]{3,2,1,0:T(8,128)(2,1)} copy(bf16[56,8,8,512]{3,1,2,0:T(8,128)(2,1)S(1)} %bitcast.67) | data formatting | bytes 7340032
  40.6 94.5 %all-gather.3.cloned.1.call-done = bf16[256,1,40,512]{3,2,1,0:T(8,128)(2,1)} async-done(((bf16[8,1,40,512]{3,2,1,0:T(8,128)(2,1)}), bf16[256,1,40,512]{3,2,1,0:T(8,128)(2,1)}) %all-gather.3.cloned.1.call-update) | async-done | bytes 10485776 | tf_op jit(solution)/shard_map/all_gather | solution.py:60
  135.1 11.3 %fusion.5 = f32[1280,448]{0,1:T(8,128)S(1)} fusion(bf16[8,1280,512]{2,1,0:T(8,128)(2,1)} %bitcast.78, bf16[8,512,448]{1,0,2:T(8,128)(2,1)} %bitcast.70), kind=kOutput, calls=%fused_computation.9 | convolution fusion | flops 4697620480 | bytes 16449536 | tf_op jit(solution)/shard_map/trc,tcf->rf/dot_general | solution.py:65
  146.5 6.6 %fusion.14 = bf16[1280,448]{0,1:T(8,128)(2,1)S(1)} fusion(bf16[8,1280,512]{2,1,0:T(8,128)(2,1)S(1)} %bitcast.79, bf16[8,512,448]{1,0,2:T(8,128)(2,1)S(1)} %bitcast.69, f32[1280,448]{0,1:T(8,128)S(1)} %fusion.5), kind=kOutput, calls=%fused_computation.12 | convolution fusion | flops 4701061120 | bytes 17596416 | tf_op jit(solution)/shard_map/trc,tcf->rf/dot_general | solution.py:68
  153.0 8.5 %convolution_convert_fusion = bf16[1280,8,512]{2,0,1:T(8,128)(2,1)} fusion(bf16[448,8,512]{2,1,0:T(8,128)(2,1)S(1)} %bitcast.68, bf16[1280,448]{0,1:T(8,128)(2,1)S(1)} %fusion.14), kind=kOutput, calls=%fused_computation.3 | convolution fusion | flops 4702863360 | bytes 15302656 | tf_op jit(solution)/shard_map/rf,ftc->trc/dot_general | solution.py:71
  161.5 0.0 reduce-scatter.5.cloned.1.call-start
  161.6 112.6 %reduce-scatter.3.cloned.1.call-done = bf16[1280,512]{1,0:T(8,128)(2,1)} async-done(((bf16[10240,512]{1,0:T(8,128)(2,1)}), bf16[1280,512]{1,0:T(8,128)(2,1)}) %reduce-scatter.3.cloned.1.call-update) | async-done | bytes 1310736 | tf_op jit(solution)/shard_map/reduce_scatter | solution.py:15
  274.2 0.0 reduce-scatter.5.cloned.1.call-update
  274.2 0.6 copy.59
  274.9 0.8 fusion.24
  275.7 0.1 broadcast_bitcast_fusion
  275.8 1.1 reshape.176
  276.9 6.9 %all-to-all-start.1 = ((f32[32,1,1280]{2,1,0:T(1,128)}), f32[32,1,1280]{2,1,0:T(1,128)S(1)}, u32[]{:S(2)}, u32[]{:S(2)}) async-start(f32[32,1,1280]{2,1,0:T(1,128)} %reshape.176), calls=%async_computation.3 | async-start | bytes 327680 | tf_op jit(solution)/shard_map/all_to_all | solution.py:21
  283.8 9.6 %all-to-all-done.1 = f32[32,1,1280]{2,1,0:T(1,128)S(1)} async-done(((f32[32,1,1280]{2,1,0:T(1,128)}), f32[32,1,1280]{2,1,0:T(1,128)S(1)}, u32[]{:S(2)}, u32[]{:S(2)}) %all-to-all-start.1) | async-done | bytes 163872 | tf_op jit(solution)/shard_map/all_to_all | solution.py:21
  293.4 0.5 broadcast.71
  293.9 1.0 reduce.10
  294.9 0.4 reshape.177
  295.3 0.1 bitcast_reduce_fusion
  295.4 0.2 copy.60
  295.6 6.8 %reduce-scatter.5.cloned.1.call-done = bf16[320,512]{1,0:T(8,128)(2,1)} async-done(((bf16[1280,512]{1,0:T(8,128)(2,1)}), bf16[320,512]{1,0:T(8,128)(2,1)}) %reduce-scatter.5.cloned.1.call-update) | async-done | bytes 327696 | tf_op jit(solution)/shard_map/reduce_scatter | solution.py:15
  302.4 1.7 maximum_bitcast_fusion
  304.1 6.2 %all-to-all-start.2 = ((bf16[8,1,40,513]{3,2,1,0:T(8,128)(2,1)}), bf16[8,1,40,513]{3,2,1,0:T(8,128)(2,1)S(1)}, u32[]{:S(2)}, u32[]{:S(2)}) async-start(bf16[8,1,40,513]{3,2,1,0:T(8,128)(2,1)} %maximum_bitcast_fusion), calls=%async_computation.4 | async-start | bytes 819200 | tf_op jit(solution)/shard_map/all_to_all | solution.py:32
  310.4 0.1 copy.62
  310.5 0.1 convert_reduce_fusion.1
  310.6 7.6 %all-to-all-done.2 = bf16[8,1,40,513]{3,2,1,0:T(8,128)(2,1)S(1)} async-done(((bf16[8,1,40,513]{3,2,1,0:T(8,128)(2,1)}), bf16[8,1,40,513]{3,2,1,0:T(8,128)(2,1)S(1)}, u32[]{:S(2)}, u32[]{:S(2)}) %all-to-all-start.2) | async-done | bytes 328352 | tf_op jit(solution)/shard_map/all_to_all | solution.py:32
  318.2 0.1 convert_reduce_fusion
  318.4 0.1 reshape.139
  318.4 2.0 gather_fusion.1
  320.4 0.1 reshape.136
  320.5 0.2 multiply_reduce_fusion.2
  320.7 0.1 mul.55
  320.9 0.1 bitcast_convert_fusion
  321.0 1.0 gather_fusion
  322.0 0.2 multiply_reduce_fusion
  322.2 0.1 reduce_sum.96
  322.3 0.1 reduce_sum.97
  322.4 0.6 broadcast_in_dim.28
  323.0 5.8 %all-to-all-start.3 = ((f32[8,1,128]{2,1,0:T(1,128)}), f32[8,1,128]{2,1,0:T(1,128)S(1)}, u32[]{:S(2)}, u32[]{:S(2)}) async-start(f32[8,1,128]{2,1,0:T(1,128)} %broadcast_in_dim.28), calls=%async_computation.5 | async-start | bytes 8192 | tf_op jit(solution)/shard_map/all_to_all | solution.py:21
  328.8 0.3 reshape.135
  329.2 6.2 %all-to-all-done.3 = f32[8,1,128]{2,1,0:T(1,128)S(1)} async-done(((f32[8,1,128]{2,1,0:T(1,128)}), f32[8,1,128]{2,1,0:T(1,128)S(1)}, u32[]{:S(2)}, u32[]{:S(2)}) %all-to-all-start.3) | async-done | bytes 4128 | tf_op jit(solution)/shard_map/all_to_all | solution.py:21
  335.3 1.1 multiply_reduce_fusion.3
  336.5 1.2 broadcast_in_dim.29
  337.7 6.2 %all-to-all-start.4 = ((f32[32,1,1]{2,1,0:T(1,128)}), f32[32,1,1]{2,1,0:T(1,128)S(1)}, u32[]{:S(2)}, u32[]{:S(2)}) async-start(f32[32,1,1]{2,1,0:T(1,128)} %broadcast_in_dim.29), calls=%async_computation.6 | async-start | bytes 32768 | tf_op jit(solution)/shard_map/all_to_all | solution.py:21
  343.9 1.4 multiply_reduce_fusion.1
  345.3 5.6 %all-to-all-done.4 = f32[32,1,1]{2,1,0:T(1,128)S(1)} async-done(((f32[32,1,1]{2,1,0:T(1,128)}), f32[32,1,1]{2,1,0:T(1,128)S(1)}, u32[]{:S(2)}, u32[]{:S(2)}) %all-to-all-start.4) | async-done | bytes 160 | tf_op jit(solution)/shard_map/all_to_all | solution.py:21
  350.9 0.6 reduce_sum.101
  (23 shorter events, 0.2 us)
Async XLA Ops:
  7.2 267.7 %copy-start = (bf16[1,448]{1,0:T(2,128)(2,1)S(1)}, bf16[1,448]{1,0:T(2,128)(2,1)}, u32[]{:S(2)}) copy-start(bf16[1,448]{1,0:T(2,128)(2,1)} %param.13) | copy-start | bytes 2692
  7.2 127.9 %all-gather.3.cloned.1.call-start = ((), (), s32[]{:S(2)}) async-start(), calls=%async_computation.9 | async-start | bytes 10813440 | tf_op jit(solution)/shard_map/all_gather | solution.py:60
  26.7 247.5 %reduce-scatter.3.cloned.1.call-start = ((), (), s32[]{:S(2)}) async-start(), calls=%async_computation.7 | async-start | bytes 11796480 | tf_op jit(solution)/shard_map/reduce_scatter | solution.py:15
  26.9 6.0 %copy-start.1 = (bf16[1,4096,448]{1,2,0:T(8,128)(2,1)S(1)}, bf16[1,4096,448]{1,2,0:T(8,128)(2,1)}, u32[]{:S(2)}) copy-start(bf16[1,4096,448]{1,2,0:T(8,128)(2,1)} %param.11) | copy-start | bytes 11010052
  32.9 3.8 %copy-start.2 = (bf16[1,448,4096]{2,1,0:T(8,128)(2,1)S(1)}, bf16[1,448,4096]{2,1,0:T(8,128)(2,1)}, u32[]{:S(2)}) copy-start(bf16[1,448,4096]{2,1,0:T(8,128)(2,1)} %param.12) | copy-start | bytes 11010052
  135.1 11.3 %copy-start.4 = (bf16[56,8,8,512]{3,2,1,0:T(8,128)(2,1)S(1)}, bf16[56,8,8,512]{3,2,1,0:T(8,128)(2,1)}, u32[]{:S(2)}) copy-start(bf16[56,8,8,512]{3,2,1,0:T(8,128)(2,1)} %copy.69) | copy-start | bytes 11010052
  135.1 11.3 %copy-start.6 = (bf16[256,1,40,512]{3,2,1,0:T(8,128)(2,1)S(1)}, bf16[256,1,40,512]{3,2,1,0:T(8,128)(2,1)}, u32[]{:S(2)}) copy-start(bf16[256,1,40,512]{3,2,1,0:T(8,128)(2,1)} %all-gather.3.cloned.1.call-done) | copy-start | bytes 31457284
  146.5 6.6 %copy-start.3 = (bf16[56,8,8,512]{3,2,1,0:T(8,128)(2,1)S(1)}, bf16[56,8,8,512]{3,2,1,0:T(8,128)(2,1)}, u32[]{:S(2)}) copy-start(bf16[56,8,8,512]{3,2,1,0:T(8,128)(2,1)} %copy.70) | copy-start | bytes 11010052
  161.5 140.9 %reduce-scatter.5.cloned.1.call-start = ((), (), s32[]{:S(2)}) async-start(), calls=%async_computation.8 | async-start | bytes 1638400 | tf_op jit(solution)/shard_map/reduce_scatter | solution.py:15
  274.9 35.5 %copy-start.5 = (s32[128,2]{0,1:T(2,128)S(1)}, s32[128,2]{0,1:T(2,128)}, u32[]{:S(2)}) copy-start(s32[128,2]{0,1:T(2,128)} %param.9) | copy-start | bytes 3076
  276.9 16.5 %all-to-all-start.1 = ((f32[32,1,1280]{2,1,0:T(1,128)}), f32[32,1,1280]{2,1,0:T(1,128)S(1)}, u32[]{:S(2)}, u32[]{:S(2)}) async-start(f32[32,1,1280]{2,1,0:T(1,128)} %reshape.176), calls=%async_computation.3 | async-start | bytes 327680 | tf_op jit(solution)/shard_map/all_to_all | solution.py:21
  304.1 14.1 %all-to-all-start.2 = ((bf16[8,1,40,513]{3,2,1,0:T(8,128)(2,1)}), bf16[8,1,40,513]{3,2,1,0:T(8,128)(2,1)S(1)}, u32[]{:S(2)}, u32[]{:S(2)}) async-start(bf16[8,1,40,513]{3,2,1,0:T(8,128)(2,1)} %maximum_bitcast_fusion), calls=%async_computation.4 | async-start | bytes 819200 | tf_op jit(solution)/shard_map/all_to_all | solution.py:32
  323.0 12.3 %all-to-all-start.3 = ((f32[8,1,128]{2,1,0:T(1,128)}), f32[8,1,128]{2,1,0:T(1,128)S(1)}, u32[]{:S(2)}, u32[]{:S(2)}) async-start(f32[8,1,128]{2,1,0:T(1,128)} %broadcast_in_dim.28), calls=%async_computation.5 | async-start | bytes 8192 | tf_op jit(solution)/shard_map/all_to_all | solution.py:21
  337.7 13.2 %all-to-all-start.4 = ((f32[32,1,1]{2,1,0:T(1,128)}), f32[32,1,1]{2,1,0:T(1,128)S(1)}, u32[]{:S(2)}, u32[]{:S(2)}) async-start(f32[32,1,1]{2,1,0:T(1,128)} %broadcast_in_dim.29), calls=%async_computation.6 | async-start | bytes 32768 | tf_op jit(solution)/shard_map/all_to_all | solution.py:21
Sparse Core Ops, SparseCore 0:
  26.8 108.2 all-gather.2
  161.7 112.4 reduce-scatter.2
  276.8 25.5 reduce-scatter.4
where the time goes:
time: 360 us
  waiting for transfers between devices  243 us (68%)
  matrix products  27.2 us (8%)
  local copies, waits for them, and re-layouts  26.6 us (7%)
  starting transfers between devices  25.4 us (7%)
  between operations  15.8 us (4%)
  blocking collectives  13.7 us (4%)
  other arithmetic  8.17 us (2%)
    reduce_scatter x2, waiting for transfers between devices, scatter_axes(): nearer = lax.psum_scatter(x, axes[0], scatter_dimension=dim, tiled=True)  119 us
    all_gather x1, waiting for transfers between devices, body(): lax.all_gather(received[None], ('tensor', 'dp'), axis=0, tiled=True)  94.5 us
    all_to_all x3, waiting for transfers between devices, copy_for_each(): return lax.all_to_all(copies, axis, split_axis=0, concat_axis=0, tiled=True)  21.4 us
    all_to_all x3, starting transfers between devices, copy_for_each(): return lax.all_to_all(copies, axis, split_axis=0, concat_axis=0, tiled=True)  18.9 us
    unnamed x22, local copies, waits for them, and re-layouts  16.1 us
    all_to_all x1, blocking collectives, body(): lax.all_to_all(send_buffer, 'expert', split_axis=0, concat_axis=0, tiled=...  13.7 us
    dot_general x1, matrix products, body(): jnp.einsum('trc,tcf->rf', block_rows, gate_weights, preferred_element_typ...  11.3 us
    dot_general x1, matrix products, body(): jnp.einsum('rf,ftc->trc', hidden, down_weights, preferred_element_type=jn...  8.47 us
  transfers between devices with their start and end apart: 7, of which 7 were waited for; matrix products, arithmetic and copies ran while one was open for 6% of the time, Pallas kernels for 0%

commit v1 on v0

v1 whole, which is shorter than its diff:
```python
import functools
import math

import jax
import jax.numpy as jnp
from jax import lax
from jax.experimental import pallas as pl
from jax.experimental.pallas import tpu as pltpu
from jax.sharding import PartitionSpec as P

D = 4096
CAP = 40
MESH = pl.DeviceIdType.MESH
NT = 8
NX = 4
F32 = jnp.float32
BF16 = jnp.bfloat16


def kernel(
    n_exp,
    tok_ref, ids_ref, gate_ref, dchk_ref, wg_hbm, wu_hbm, wd_hbm,
    out_ref, res_ref, alarm_ref,
    wg, wu, wd, x, p, acc_ga, acc_ua, acc_gb, acc_ub, hid, fin,
    sbuf, rbuf, bbuf, qbuf,
    xh, xf, zh, zf, yh, yf, bh, bf,
    cs, cr, cf, cc, ds, dr, es, er, gs, gr,
    w_sem, d_s, d_r,
    a1f_s, a1f_r, a1h_s, a1h_r, a2f_s, a2f_r, a2h_s, a2h_r,
    b1f_s, b1f_r, b1h_s, b1h_r, b2f_s, b2f_r, b2h_s, b2h_r,
    xh_s, xh_r, xf_s, xf_r, zh_s, zh_r, zf_s, zf_r,
    yh_s, yh_r, yf_s, yf_r, bh_s, bh_r, bf_s, bf_r,
    c_s, c_r, cc_s, cc_r, q_s, q_r, ds_s, ds_r, es_s, es_r, gs_s, gs_r,
):
    e = lax.axis_index("expert")
    t = lax.axis_index("tensor")
    d = lax.axis_index("dp")
    rows = x.shape[2]
    cols = x.shape[3]
    ff = wg.shape[2]
    toks = tok_ref.shape[0]
    na = rows * 3 // 5
    nb = rows - na
    A, A0, A1 = pl.ds(0, na), pl.ds(0, na // 2), pl.ds(na // 2, na // 2)
    B, B0, B1 = pl.ds(na, nb), pl.ds(na, nb // 2), pl.ds(na + nb // 2, nb // 2)

    def tz(o):
        return lax.rem(t + (o + 2 * NT), NT)

    def dx(o):
        return lax.rem(d + (o + 2 * NX), NX)

    def ex(o):
        return lax.rem(e + o, n_exp)

    zdev = ((e, tz(1), d), (e, tz(-1), d))
    xdev = ((e, t, dx(1)), (e, t, dx(-1)))

    def copy(src, dst, ssem, rsem, dev):
        return pltpu.make_async_remote_copy(
            src_ref=src, dst_ref=dst, send_sem=ssem, recv_sem=rsem,
            device_id=dev, device_id_type=MESH,
        )

    def send(src, dst, ssem, rsem, dev):
        copy(src, dst, ssem, rsem, dev).start()

    def got(dst, ssem, rsem):
        copy(dst, dst, ssem, rsem, xdev[0]).wait_recv()

    def sent(src, ssem, rsem):
        copy(src, src, ssem, rsem, xdev[0]).wait_send()

    def off(k):
        if isinstance(k, int):
            h, odd, last = (k + 1) // 2, k % 2, k // 7
        else:
            h, odd, last = lax.div(k + 1, 2), lax.rem(k, 2), lax.div(k, 7)
        return h - 2 * h * odd * (1 - last)

    w_copies = [
        pltpu.make_async_copy(wg_hbm, wg, w_sem.at[0]),
        pltpu.make_async_copy(wu_hbm, wu, w_sem.at[1]),
    ] + [
        pltpu.make_async_copy(wd_hbm.at[:, pl.ds(i * cols, cols)], wd.at[i], w_sem.at[2 + i])
        for i in range(NT)
    ]
    for c in w_copies:
        c.start()
    barrier = pltpu.get_barrier_semaphore()
    for o in range(1, n_exp):
        pl.semaphore_signal(barrier, inc=1, device_id=(ex(o), t, d), device_id_type=MESH)
    for o in range(1, NT):
        pl.semaphore_signal(barrier, inc=1, device_id=(e, tz(o), d), device_id_type=MESH)
    for o in range(1, NX):
        pl.semaphore_signal(barrier, inc=1, device_id=(e, t, dx(o)), device_id_type=MESH)

    ids = ids_ref[...].astype(F32)
    ids_row = [jnp.transpose(jnp.broadcast_to(ids[:, k : k + 1], (toks, toks)))[0:8] for k in range(2)]
    iota_e = lax.broadcasted_iota(jnp.int32, (8, toks), 0).astype(F32)
    count = (ids_row[0] == iota_e).astype(F32) + (ids_row[1] == iota_e).astype(F32)
    above = lax.broadcasted_iota(jnp.int32, (toks, toks), 0) < lax.broadcasted_iota(jnp.int32, (toks, toks), 1)
    before = jnp.dot(count.astype(BF16), above.astype(F32).astype(BF16), preferred_element_type=F32)
    place = jnp.where(count > 0.5, before, -1.0)
    iota_p = lax.broadcasted_iota(jnp.int32, (CAP, toks), 0).astype(F32)
    pick = jnp.concatenate(
        [(iota_p == jnp.broadcast_to(place[i : i + 1], (CAP, toks))).astype(F32) for i in range(n_exp)], axis=0
    )
    slot_rows = jnp.dot(pick.astype(BF16), tok_ref[...], preferred_element_type=F32)
    sbuf[...] = slot_rows.reshape(n_exp, CAP, cols).astype(BF16)

    pl.semaphore_wait(barrier, n_exp - 1 + NT - 1 + NX - 1)

    for o in range(1, n_exp):
        send(sbuf.at[ex(o)], rbuf.at[e], d_s.at[o - 1], d_r.at[o - 1], (ex(o), t, d))
    rbuf[e] = sbuf[e]
    acc_ga[...] = jnp.zeros_like(acc_ga)
    acc_ua[...] = jnp.zeros_like(acc_ua)
    acc_gb[...] = jnp.zeros_like(acc_gb)
    acc_ub[...] = jnp.zeros_like(acc_ub)
    for o in range(1, n_exp):
        got(rbuf.at[ex(n_exp - o)], d_s.at[o - 1], d_r.at[o - 1])
    x[t, d] = rbuf[...].astype(F32).reshape(rows, cols).astype(BF16)

    def mul_a(tp, dp):
        v = x[tp, dp, A, :]
        acc_ga[dp] += jnp.dot(v, wg[tp], preferred_element_type=F32)
        acc_ua[dp] += jnp.dot(v, wu[tp], preferred_element_type=F32)

    def mul_b(tp):
        v = x[tp, :, B, :].reshape(NX * nb, cols)
        acc_gb[...] += jnp.dot(v, wg[tp], preferred_element_type=F32)
        acc_ub[...] += jnp.dot(v, wu[tp], preferred_element_type=F32)

    def silu(g, u):
        return (g / (1.0 + jnp.exp(-g)) * u).astype(BF16)

    def act_a(dp):
        hid[dp, A, :] = silu(acc_ga[dp], acc_ua[dp])

    def a1_send(s):
        if s < 4:
            send(x.at[tz(1 - s), d, A], x.at[tz(1 - s), d, A], a1f_s.at[s - 1, 0], a1f_r.at[s - 1, 0], zdev[0])
            send(x.at[tz(s - 1), d, A], x.at[tz(s - 1), d, A], a1f_s.at[s - 1, 1], a1f_r.at[s - 1, 1], zdev[1])
        else:
            send(x.at[tz(-3), d, A0], x.at[tz(-3), d, A0], a1h_s.at[0], a1h_r.at[0], zdev[0])
            send(x.at[tz(3), d, A1], x.at[tz(3), d, A1], a1h_s.at[1], a1h_r.at[1], zdev[1])

    def a1_got(s):
        if s < 4:
            got(x.at[tz(-s), d, A], a1f_s.at[s - 1, 0], a1f_r.at[s - 1, 0])
            got(x.at[tz(s), d, A], a1f_s.at[s - 1, 1], a1f_r.at[s - 1, 1])
        else:
            got(x.at[tz(4), d, A0], a1h_s.at[0], a1h_r.at[0])
            got(x.at[tz(4), d, A1], a1h_s.at[1], a1h_r.at[1])

    def a2_send(k):
        tp = tz(off(k))
        for i in range(2):
            send(x.at[tp, d, A], x.at[tp, d, A], a2f_s.at[k, i], a2f_r.at[k, i], xdev[i])

    def b2_send(s):
        if s < 4:
            send(x.at[tz(1 - s), :, B], x.at[tz(1 - s), :, B], b2f_s.at[s - 1, 0], b2f_r.at[s - 1, 0], zdev[0])
            send(x.at[tz(s - 1), :, B], x.at[tz(s - 1), :, B], b2f_s.at[s - 1, 1], b2f_r.at[s - 1, 1], zdev[1])
        else:
            send(x.at[tz(-3), :, B0], x.at[tz(-3), :, B0], b2h_s.at[0], b2h_r.at[0], zdev[0])
            send(x.at[tz(3), :, B1], x.at[tz(3), :, B1], b2h_s.at[1], b2h_r.at[1], zdev[1])

    def b2_got(s):
        if s < 4:
            got(x.at[tz(-s), :, B], b2f_s.at[s - 1, 0], b2f_r.at[s - 1, 0])
            got(x.at[tz(s), :, B], b2f_s.at[s - 1, 1], b2f_r.at[s - 1, 1])
        else:
            got(x.at[tz(4), :, B0], b2h_s.at[0], b2h_r.at[0])
            got(x.at[tz(4), :, B1], b2h_s.at[1], b2h_r.at[1])

    def pass_on(k, carry):
        tp = tz(off(k))
        got(x.at[tp, dx(-1), A], a2f_s.at[k, 0], a2f_r.at[k, 0])
        send(x.at[tp, dx(-1), A0], x.at[tp, dx(-1), A0], a2h_s.at[k, 0], a2h_r.at[k, 0], xdev[0])
        got(x.at[tp, dx(1), A], a2f_s.at[k, 1], a2f_r.at[k, 1])
        send(x.at[tp, dx(1), A1], x.at[tp, dx(1), A1], a2h_s.at[k, 1], a2h_r.at[k, 1], xdev[1])
        mul_a(tp, dx(-1))
        mul_a(tp, dx(1))
        return carry

    def far_side(k, carry):
        tp = tz(off(k))
        got(x.at[tp, dx(2), A0], a2h_s.at[k, 0], a2h_r.at[k, 0])
        got(x.at[tp, dx(2), A1], a2h_s.at[k, 1], a2h_r.at[k, 1])
        mul_a(tp, dx(2))
        return carry

    a1_send(1)
    for i in range(2):
        send(x.at[t, d, B], x.at[t, d, B], b1f_s.at[i], b1f_r.at[i], xdev[i])
    a2_send(0)
    w_copies[0].wait()
    w_copies[1].wait()
    mul_a(t, d)
    got(x.at[t, dx(-1), B], b1f_s.at[0], b1f_r.at[0])
    send(x.at[t, dx(-1), B0], x.at[t, dx(-1), B0], b1h_s.at[0], b1h_r.at[0], xdev[0])
    got(x.at[t, dx(1), B], b1f_s.at[1], b1f_r.at[1])
    send(x.at[t, dx(1), B1], x.at[t, dx(1), B1], b1h_s.at[1], b1h_r.at[1], xdev[1])
    a1_got(1)
    a1_send(2)
    a2_send(1)
    a2_send(2)
    mul_a(tz(-1), d)
    mul_a(tz(1), d)
    got(x.at[t, dx(2), B0], b1h_s.at[0], b1h_r.at[0])
    got(x.at[t, dx(2), B1], b1h_s.at[1], b1h_r.at[1])
    b2_send(1)
    mul_b(t)
    a1_got(2)
    a1_send(3)
    a2_send(3)
    a2_send(4)
    mul_a(tz(-2), d)
    mul_a(tz(2), d)
    a1_got(3)
    a1_send(4)
    a2_send(5)
    a2_send(6)
    mul_a(tz(-3), d)
    mul_a(tz(3), d)
    a1_got(4)
    a2_send(7)
    mul_a(tz(4), d)
    act_a(d)
    lax.fori_loop(0, 5, pass_on, 0)
    b2_got(1)
    b2_send(2)
    mul_b(tz(-1))
    mul_b(tz(1))
    lax.fori_loop(5, 8, pass_on, 0)
    b2_got(2)
    b2_send(3)
    mul_b(tz(-2))
    mul_b(tz(2))
    act_a(dx(-1))
    act_a(dx(1))
    lax.fori_loop(0, 6, far_side, 0)
    b2_got(3)
    b2_send(4)
    mul_b(tz(-3))
    mul_b(tz(3))
    lax.fori_loop(6, 8, far_side, 0)
    act_a(dx(2))
    b2_got(4)
    mul_b(tz(4))
    hb = silu(acc_gb[...], acc_ub[...])
    for i in range(NX):
        hid[i, B, :] = hb[i * nb : (i + 1) * nb]

    for c in w_copies[2:]:
        c.wait()

    def down(tp):
        def one(dp, carry):
            p[tp, dp] = jnp.dot(hid[dp], wd[tp], preferred_element_type=F32).astype(BF16)
            return carry

        lax.fori_loop(0, NX, one, 0)

    def add(ref, tp, dp, span, *others):
        total = ref[tp, dp, span, :].astype(F32)
        for o in others:
            total = total + o.astype(F32)
        ref[tp, dp, span, :] = total.astype(BF16)

    def xo(j):
        return off(7 - j)

    def x_first(j):
        tp = tz(xo(j))
        down(tp)
        send(p.at[tp, dx(2), A1], xh.at[j, 0], xh_s.at[j, 0], xh_r.at[j, 0], xdev[0])
        send(p.at[tp, dx(2), A0], xh.at[j, 1], xh_s.at[j, 1], xh_r.at[j, 1], xdev[1])

    def x_second(j, carry):
        tp = tz(xo(j))
        got(xh.at[j, 0], xh_s.at[j, 0], xh_r.at[j, 0])
        add(p, tp, dx(1), A1, xh[j, 0])
        send(p.at[tp, dx(1), A], xf.at[j, 0], xf_s.at[j, 0], xf_r.at[j, 0], xdev[0])
        got(xh.at[j, 1], xh_s.at[j, 1], xh_r.at[j, 1])
        add(p, tp, dx(-1), A0, xh[j, 1])
        send(p.at[tp, dx(-1), A], xf.at[j, 1], xf_s.at[j, 1], xf_r.at[j, 1], xdev[1])
        return carry

    def x_third(j):
        tp = tz(xo(j))
        got(xf.at[j, 0], xf_s.at[j, 0], xf_r.at[j, 0])
        got(xf.at[j, 1], xf_s.at[j, 1], xf_r.at[j, 1])
        add(p, tp, d, A, xf[j, 0], xf[j, 1])

    def z_first():
        send(p.at[tz(4), d, A1], zh.at[0], zh_s.at[0], zh_r.at[0], zdev[0])
        send(p.at[tz(4), d, A0], zh.at[1], zh_s.at[1], zh_r.at[1], zdev[1])

    def z_step(s):
        if s == 1:
            got(zh.at[0], zh_s.at[0], zh_r.at[0])
            add(p, tz(3), d, A1, zh[0])
            got(zh.at[1], zh_s.at[1], zh_r.at[1])
            add(p, tz(-3), d, A0, zh[1])
        else:
            got(zf.at[s - 2, 0], zf_s.at[s - 2, 0], zf_r.at[s - 2, 0])
            add(p, tz(4 - s), d, A, zf[s - 2, 0])
            got(zf.at[s - 2, 1], zf_s.at[s - 2, 1], zf_r.at[s - 2, 1])
            add(p, tz(s - 4), d, A, zf[s - 2, 1])
        send(p.at[tz(4 - s), d, A], zf.at[s - 1, 0], zf_s.at[s - 1, 0], zf_r.at[s - 1, 0], zdev[0])
        send(p.at[tz(s - 4), d, A], zf.at[s - 1, 1], zf_s.at[s - 1, 1], zf_r.at[s - 1, 1], zdev[1])

    def y_first():
        send(p.at[tz(4), :, B1], yh.at[0], yh_s.at[0], yh_r.at[0], zdev[0])
        send(p.at[tz(4), :, B0], yh.at[1], yh_s.at[1], yh_r.at[1], zdev[1])

    def y_step(s):
        if s == 1:
            got(yh.at[0], yh_s.at[0], yh_r.at[0])
            add(p, tz(3), slice(None), B1, yh[0])
            got(yh.at[1], yh_s.at[1], yh_r.at[1])
            add(p, tz(-3), slice(None), B0, yh[1])
        else:
            got(yf.at[s - 2, 0], yf_s.at[s - 2, 0], yf_r.at[s - 2, 0])
            add(p, tz(4 - s), slice(None), B, yf[s - 2, 0])
            got(yf.at[s - 2, 1], yf_s.at[s - 2, 1], yf_r.at[s - 2, 1])
            add(p, tz(s - 4), slice(None), B, yf[s - 2, 1])
        send(p.at[tz(4 - s), :, B], yf.at[s - 1, 0], yf_s.at[s - 1, 0], yf_r.at[s - 1, 0], zdev[0])
        send(p.at[tz(s - 4), :, B], yf.at[s - 1, 1], yf_s.at[s - 1, 1], yf_r.at[s - 1, 1], zdev[1])

    x_first(0)
    y_first()
    x_first(1)
    x_first(2)
    x_second(0, 0)
    y_step(1)
    x_first(3)
    x_first(4)
    lax.fori_loop(1, 3, x_second, 0)
    x_first(5)
    x_first(6)
    x_first(7)

    dc = jnp.broadcast_to(dchk_ref[...].astype(F32), (16, ff)).astype(BF16)
    for i in range(NX):
        part = lax.dot_general(dc, hid[i], (((1,), (1,)), ((), ())), preferred_element_type=F32)
        cs[i] = part[0:8]
    for o in range(1, NX):
        send(cs.at[dx(o)], cr.at[o - 1], c_s.at[o - 1], c_r.at[o - 1], (e, t, dx(o)))

    lax.fori_loop(3, 5, x_second, 0)
    x_third(0)
    z_first()
    y_step(2)
    lax.fori_loop(5, 8, x_second, 0)
    x_third(1)
    x_third(2)
    z_step(1)
    y_step(3)
    for o in range(1, NX):
        got(cr.at[o - 1], c_s.at[o - 1], c_r.at[o - 1])
    cf[...] = cs[d] + cr[0] + cr[1] + cr[2]
    cc[e] = cf[...]
    for o in range(1, n_exp):
        send(cf, cc.at[e], cc_s.at[o - 1], cc_r.at[o - 1], (ex(o), t, d))
    x_third(3)
    x_third(4)
    z_step(2)
    got(yf.at[2, 0], yf_s.at[2, 0], yf_r.at[2, 0])
    got(yf.at[2, 1], yf_s.at[2, 1], yf_r.at[2, 1])
    add(p, t, slice(None), B, yf[2, 0], yf[2, 1])
    send(p.at[t, dx(2), B1], bh.at[0], bh_s.at[0], bh_r.at[0], xdev[0])
    send(p.at[t, dx(2), B0], bh.at[1], bh_s.at[1], bh_r.at[1], xdev[1])
    x_third(5)
    x_third(6)
    z_step(3)
    got(bh.at[0], bh_s.at[0], bh_r.at[0])
    add(p, t, dx(1), B1, bh[0])
    send(p.at[t, dx(1), B], bf.at[0], bf_s.at[0], bf_r.at[0], xdev[0])
    got(bh.at[1], bh_s.at[1], bh_r.at[1])
    add(p, t, dx(-1), B0, bh[1])
    send(p.at[t, dx(-1), B], bf.at[1], bf_s.at[1], bf_r.at[1], xdev[1])
    x_third(7)

    iota_l = lax.broadcasted_iota(jnp.int32, (toks, toks), 1).astype(F32)
    left = [(ids[:, k : k + 1] == iota_l).astype(F32) for k in range(2)]
    below = lax.broadcasted_iota(jnp.int32, (toks, toks), 1) < lax.broadcasted_iota(jnp.int32, (toks, toks), 0)
    before_col = jnp.dot(
        below.astype(F32).astype(BF16), (left[0] + left[1]).astype(BF16), preferred_element_type=F32
    )
    pos = [jnp.sum(left[k] * before_col, axis=1, keepdims=True) for k in range(2)]
    gates = gate_ref[...].astype(F32)
    gate_sum = gates[:, 0:1] + gates[:, 1:2]
    weight = [gates[:, k : k + 1] / gate_sum for k in range(2)]
    iota_s = lax.broadcasted_iota(jnp.int32, (toks, rows), 1).astype(F32)
    mine = (e * CAP).astype(F32)

    for o in range(1, n_exp):
        got(cc.at[ex(n_exp - o)], cc_s.at[o - 1], cc_r.at[o - 1])
    check = jnp.zeros((toks, 1), F32)
    for k in range(2):
        row = jnp.zeros((toks, rows), F32)
        for i in range(n_exp):
            row = row + jnp.where(ids[:, k : k + 1] == float(i), jnp.broadcast_to(cc[i, 0:1, :], (toks, rows)), 0.0)
        picked = jnp.where(iota_s == pos[k] + mine, row, 0.0)
        check = check + weight[k] * jnp.sum(picked, axis=1, keepdims=True)

    got(zf.at[2, 0], zf_s.at[2, 0], zf_r.at[2, 0])
    got(zf.at[2, 1], zf_s.at[2, 1], zf_r.at[2, 1])
    fin[A, :] = p[t, d, A, :].astype(F32) + zf[2, 0].astype(F32) + zf[2, 1].astype(F32)
    got(bf.at[0], bf_s.at[0], bf_r.at[0])
    got(bf.at[1], bf_s.at[1], bf_r.at[1])
    fin[B, :] = p[t, d, B, :].astype(F32) + bf[0].astype(F32) + bf[1].astype(F32)

    bbuf[...] = fin[...].reshape(n_exp, CAP, cols).astype(BF16)
    for o in range(1, n_exp):
        send(bbuf.at[ex(o)], qbuf.at[e], q_s.at[o - 1], q_r.at[o - 1], (ex(o), t, d))
    qbuf[e] = bbuf[e]
    for o in range(1, n_exp):
        got(qbuf.at[ex(n_exp - o)], q_s.at[o - 1], q_r.at[o - 1])
    back = qbuf[...].astype(F32).reshape(rows, cols).astype(BF16)
    combined = jnp.zeros((toks, cols), F32)
    for k in range(2):
        sel = (iota_s == ids[:, k : k + 1] * float(CAP) + pos[k]).astype(F32).astype(BF16)
        combined = combined + weight[k] * jnp.dot(sel, back, preferred_element_type=F32)
    out_ref[...] = combined
    diff = jnp.sum(combined, axis=1, keepdims=True) - check
    diff_row = jnp.transpose(jnp.broadcast_to(diff, (toks, toks)))[0:8]

    ds[...] = diff_row
    for o in range(1, NT):
        send(ds, dr.at[t], ds_s.at[o - 1], ds_r.at[o - 1], (e, tz(o), d))
    dr[t] = diff_row
    for o in range(1, NT):
        got(dr.at[tz(-o)], ds_s.at[o - 1], ds_r.at[o - 1])
    total = dr[0]
    for i in range(1, NT):
        total = total + dr[i]
    residual = total * (1.0 / math.sqrt(D))
    res_ref[...] = residual[0:1]
    score = jnp.broadcast_to(jnp.sum(residual * residual, axis=1, keepdims=True), (8, toks))
    es[...] = score
    for o in range(1, NX):
        send(es, er.at[d], es_s.at[o - 1], es_r.at[o - 1], (e, t, dx(o)))
    er[d] = score
    for o in range(1, NX):
        got(er.at[dx(-o)], es_s.at[o - 1], es_r.at[o - 1])
    score = er[0]
    for i in range(1, NX):
        score = score + er[i]
    gs[...] = score
    for o in range(1, n_exp):
        send(gs, gr.at[e], gs_s.at[o - 1], gs_r.at[o - 1], (ex(o), t, d))
    gr[e] = score
    for o in range(1, n_exp):
        got(gr.at[ex(n_exp - o)], gs_s.at[o - 1], gs_r.at[o - 1])
    score = gr[0]
    for i in range(1, n_exp):
        score = score + gr[i]
    alarm_ref[...] = score[0:1, 0:1] * (1.0 / (toks * n_exp * NX))

    for o in range(n_exp - 1):
        sent(sbuf.at[0], d_s.at[o], d_r.at[o])
        sent(cf, cc_s.at[o], cc_r.at[o])
        sent(bbuf.at[0], q_s.at[o], q_r.at[o])
        sent(gs, gs_s.at[o], gs_r.at[o])
    for o in range(NX - 1):
        sent(cs.at[0], c_s.at[o], c_r.at[o])
        sent(es, es_s.at[o], es_r.at[o])
    for o in range(NT - 1):
        sent(ds, ds_s.at[o], ds_r.at[o])
    for i in range(2):
        for s in range(3):
            sent(x.at[t, d, A], a1f_s.at[s, i], a1f_r.at[s, i])
            sent(x.at[t, :, B], b2f_s.at[s, i], b2f_r.at[s, i])
            sent(p.at[t, d, A], zf_s.at[s, i], zf_r.at[s, i])
            sent(p.at[t, :, B], yf_s.at[s, i], yf_r.at[s, i])
        sent(x.at[t, d, A0], a1h_s.at[i], a1h_r.at[i])
        sent(x.at[t, d, B], b1f_s.at[i], b1f_r.at[i])
        sent(x.at[t, d, B0], b1h_s.at[i], b1h_r.at[i])
        sent(x.at[t, :, B0], b2h_s.at[i], b2h_r.at[i])
        sent(p.at[t, d, A0], zh_s.at[i], zh_r.at[i])
        sent(p.at[t, :, B0], yh_s.at[i], yh_r.at[i])
        sent(p.at[t, d, B0], bh_s.at[i], bh_r.at[i])
        sent(p.at[t, d, B], bf_s.at[i], bf_r.at[i])

        def drain(k, carry):
            sent(x.at[t, d, A], a2f_s.at[k, i], a2f_r.at[k, i])
            sent(x.at[t, d, A0], a2h_s.at[k, i], a2h_r.at[k, i])
            sent(p.at[t, d, A0], xh_s.at[k, i], xh_r.at[k, i])
            sent(p.at[t, d, A], xf_s.at[k, i], xf_r.at[k, i])
            return carry

        lax.fori_loop(0, NT, drain, 0)


def body(tokens, expert_ids, gate_fixed, w_gate, w_up, w_down, down_check):
    n_exp = lax.axis_size("expert")
    toks, cols = tokens.shape
    ff = w_gate.shape[2]
    rows = n_exp * CAP
    na = rows * 3 // 5
    nb = rows - na
    dma = lambda *s: pltpu.SemaphoreType.DMA(s)
    both = lambda *s: [dma(*s), dma(*s)]
    vm = pltpu.VMEM
    scratch = [
        vm((NT, cols, ff), BF16), vm((NT, cols, ff), BF16), vm((NT, ff, cols), BF16),
        vm((NT, NX, rows, cols), BF16), vm((NT, NX, rows, cols), BF16),
        vm((NX, na, ff), F32), vm((NX, na, ff), F32), vm((NX * nb, ff), F32), vm((NX * nb, ff), F32),
        vm((NX, rows, ff), BF16), vm((rows, cols), F32),
        vm((n_exp, CAP, cols), BF16), vm((n_exp, CAP, cols), BF16),
        vm((n_exp, CAP, cols), BF16), vm((n_exp, CAP, cols), BF16),
        vm((NT, 2, na // 2, cols), BF16), vm((NT, 2, na, cols), BF16),
        vm((2, na // 2, cols), BF16), vm((3, 2, na, cols), BF16),
        vm((2, NX, nb // 2, cols), BF16), vm((3, 2, NX, nb, cols), BF16),
        vm((2, nb // 2, cols), BF16), vm((2, nb, cols), BF16),
        vm((NX, 8, rows), F32), vm((NX - 1, 8, rows), F32), vm((8, rows), F32), vm((n_exp, 8, rows), F32),
        vm((8, toks), F32), vm((NT, 8, toks), F32), vm((8, toks), F32), vm((NX, 8, toks), F32),
        vm((8, toks), F32), vm((n_exp, 8, toks), F32),
        dma(2 + NT), *both(n_exp - 1),
        *both(3, 2), *both(2), *both(NT, 2), *both(NT, 2),
        *both(2), *both(2), *both(3, 2), *both(2),
        *both(NT, 2), *both(NT, 2), *both(2), *both(3, 2),
        *both(2), *both(3, 2), *both(2), *both(2),
        *both(NX - 1), *both(n_exp - 1), *both(n_exp - 1), *both(NT - 1), *both(NX - 1), *both(n_exp - 1),
    ]
    vmem = pl.BlockSpec(memory_space=pltpu.VMEM)
    hbm = pl.BlockSpec(memory_space=pl.ANY)
    mix, residual, alarm = pl.pallas_call(
        functools.partial(kernel, n_exp),
        out_shape=(
            jax.ShapeDtypeStruct((toks, cols), F32),
            jax.ShapeDtypeStruct((1, toks), F32),
            jax.ShapeDtypeStruct((1, 1), F32),
        ),
        in_specs=[vmem, vmem, vmem, vmem, hbm, hbm, hbm],
        out_specs=(vmem, vmem, vmem),
        scratch_shapes=scratch,
        compiler_params=pltpu.CompilerParams(
            collective_id=0, has_side_effects=True, vmem_limit_bytes=66_000_000
        ),
    )(
        tokens, expert_ids, gate_fixed, down_check,
        w_gate.reshape(NT, cols, ff), w_up.reshape(NT, cols, ff), w_down.reshape(ff, NT * cols),
    )
    return mix, residual.reshape(toks), alarm.reshape(())


def solution(mesh):
    return jax.shard_map(
        body,
        mesh=mesh,
        in_specs=(
            P(("expert", "dp"), "tensor"),
            P(("expert", "dp"), None),
            P(("expert", "dp"), None),
            P("expert", None, ("tensor", "dp")),
            P("expert", None, ("tensor", "dp")),
            P("expert", ("tensor", "dp"), None),
            P("expert", ("tensor", "dp")),
        ),
        out_specs=(P(("expert", "dp"), "tensor"), P(("expert", "dp")), P()),
        check_vma=False,
    )
```

time: 360 us -> 187 us (0.52)
  waiting for transfers between devices: 243 us -> 0 us
  Pallas kernels: 0 us -> 165 us
  matrix products: 27.2 us -> 0 us
  starting transfers between devices: 25.4 us -> 0 us
  blocking collectives: 13.7 us -> 0 us
  between operations: 15.8 us -> 2.45 us
  other arithmetic: 8.17 us -> 0 us
  local copies, waits for them, and re-layouts: 26.6 us -> 18.5 us
    pallas_call x0 -> x1, Pallas kernels: none -> 165 us  [body(): pl.pallas_call(functools.partial(kernel, n_exp), out_shape=(jax.ShapeDtyp...]
    reduce_scatter x2 -> x0, waiting for transfers between devices: 119 us -> none  [scatter_axes(): nearer = lax.psum_scatter(x, axes[0], scatter_dimension=dim, tiled=True)]
    all_gather x1 -> x0, waiting for transfers between devices: 94.5 us -> none  [body(): lax.all_gather(received[None], ('tensor', 'dp'), axis=0, tiled=True)]
    all_to_all x4 -> x0, waiting for transfers between devices: 29 us -> none  [the longest x3 21.4 us: copy_for_each(): return lax.all_to_all(copies, axis, split_axis=0, concat_axis=0, tiled=True)]
    dot_general x4 -> x0, matrix products: 27.2 us -> none  [the longest x1 11.3 us: body(): jnp.einsum('trc,tcf->rf', block_rows, gate_weights, preferred_element_typ...]
    all_to_all x4 -> x0, starting transfers between devices: 25.1 us -> none  [the longest x3 18.9 us: copy_for_each(): return lax.all_to_all(copies, axis, split_axis=0, concat_axis=0, tiled=True)]
    all_to_all x1 -> x0, blocking collectives: 13.7 us -> none  [body(): lax.all_to_all(send_buffer, 'expert', split_axis=0, concat_axis=0, tiled=...]
    reduce_sum x10 -> x0, other arithmetic: 3.88 us -> none  [the longest x1 1.41 us: body(): combined = jnp.sum(picked * weights[:, :, None], axis=1)]
  transfers between devices with their start and end apart: 7 -> 0, of which waited for: 7 -> 0; matrix products, arithmetic and copies ran while one was open for 6% -> 0% of each run, Pallas kernels for 0% -> 0%
where the time goes in v1:
time: 187 us; the launch traced here: 186 us
  Pallas kernels  165 us (88%)
  local copies, waits for them, and re-layouts  18.5 us (10%)
  between operations  2.45 us (1%)
    pallas_call x1, Pallas kernels, body(): pl.pallas_call(functools.partial(kernel, n_exp), out_shape=(jax.ShapeDtyp...  165 us
    unnamed x6, local copies, waits for them, and re-layouts  18.5 us

profile of v1, /device:TPU:1, one launch (start us, length us, event | category | flops | bytes accessed | tf_op | source)
XLA Modules:
  0.0 186.3 jit_solution(7290545056968579913)
XLA Ops:
  0.6 1.4 copy.12.ids_ref
  2.0 1.4 copy.13.gate_ref
  3.4 6.4 %copy.10 = bf16[1,4096,448]{2,1,0:T(8,128)(2,1)} copy(bf16[1,4096,448]{1,2,0:T(8,128)(2,1)} %param.10) | data formatting | bytes 7340032 | tf_op args[3]
  9.8 6.5 %copy.11 = bf16[1,4096,448]{2,1,0:T(8,128)(2,1)} copy(bf16[1,4096,448]{1,2,0:T(8,128)(2,1)} %param.11) | data formatting | bytes 7340032 | tf_op args[4]
  16.3 165.3 %shard_map.94 = (f32[128,512]{1,0:T(8,128)}, f32[1,128]{1,0:T(1,128)}, f32[1,1]{1,0:T(1,128)}) custom-call(bf16[128,512]{1,0:T(8,128)(2,1)} %tok_ref.1, s32[128,2]{1,0:T(8,128)} %copy.12.ids_ref, s32[128,2]{1,0:T(8,128)} %copy.13.gate_ref, bf16[1,448]{1,0:T(2,128)(2,1)} %dchk_ref.1, bf16[8,512,448]{2,1,0:T(8,128)(2,1)} %bitcast.5, ...), custom_call_target="tpu_custom_call" | custom-call | tf_op jit(solution)/shard_map/pallas_call | solution.py:533
  181.6 1.7 copy.17
  183.3 1.2 copy.18

commit v2 on v0

v2 whole, which is shorter than its diff:
```python
import functools
import math

import jax
import jax.numpy as jnp
from jax import lax
from jax.experimental import pallas as pl
from jax.experimental.pallas import tpu as pltpu
from jax.sharding import PartitionSpec as P

D = 4096
CAP = 40
MESH = pl.DeviceIdType.MESH
NT = 8
NX = 4
MESSAGES = 164
F32 = jnp.float32
BF16 = jnp.bfloat16

GATHER = (
    ("ca", 0, 0), ("b1", 0, 0, 1), ("b1", 1, 1, 1), ("a1", 0, 0, 1), ("a1", 1, 1, 1), ("b1", 0, 1, 1),
    ("b1", 1, 0, 1), ("a1", 0, 1, 1), ("a1", 1, 0, 1), ("ca", 1, 0), ("ca", 2, 0), ("a2", 0, 0, 0, 1),
    ("a2", 1, 0, 1, 1), ("a1", 0, 0, 2), ("a1", 1, 1, 2), ("a2", 0, 0, 1, 1), ("a2", 1, 0, 0, 1), ("ca", 0, -1),
    ("ca", 0, 1), ("b1", 0, 0, 2), ("b1", 1, 1, 2), ("b2",), ("a1", 0, 1, 2), ("a1", 1, 0, 2), ("cb", 0),
    ("ca", 3, 0), ("ca", 4, 0), ("a1", 0, 0, 3), ("a1", 1, 1, 3), ("a2", 0, 1, 0, 1), ("a2", 1, 1, 0, 1),
    ("a2", 0, 2, 1, 1), ("a2", 1, 2, 1, 1), ("a2", 0, 1, 1, 1), ("a2", 1, 1, 1, 1), ("ca", 1, -1), ("ca", 1, 1),
    ("b2", 0, 0, 1), ("b2", 1, 1, 1), ("a2", 0, 2, 0, 1), ("a2", 1, 2, 0, 1), ("ca", 2, -1), ("ca", 2, 1),
    ("a2", 0, 0, 0, 2), ("a2", 1, 0, 1, 2), ("ca", 0, 2), ("a2", 0, 3, 0, 1), ("a2", 1, 3, 0, 1), ("b2", 0, 1, 1),
    ("b2", 1, 0, 1), ("cb", 1), ("a2", 0, 4, 1, 1), ("a2", 1, 4, 1, 1), ("cb", 2), ("a1", 0, 1, 3), ("a1", 1, 0, 3),
    ("ca", 5, 0), ("a2", 0, 3, 1, 1), ("a2", 1, 3, 1, 1), ("ca", 3, -1), ("ca", 3, 1), ("a1", 0, 0, 4),
    ("a1", 1, 1, 4), ("ca", 6, 0), ("ca", 7, 0), ("a2", 0, 4, 0, 1), ("a2", 1, 4, 0, 1), ("ca", 4, -1), ("ca", 4, 1),
    ("act", 0), ("a2", 0, 5, 0, 1), ("a2", 1, 5, 0, 1), ("a2", 0, 6, 1, 1), ("a2", 1, 6, 1, 1), ("b2", 0, 0, 2),
    ("b2", 1, 1, 2), ("a2", 0, 1, 0, 2), ("a2", 1, 2, 1, 2), ("a2", 1, 1, 1, 2), ("a2", 0, 2, 0, 2), ("ca", 1, 2),
    ("ca", 2, 2), ("b2", 0, 1, 2), ("b2", 1, 0, 2), ("cb", 3), ("a2", 0, 3, 0, 2), ("a2", 1, 4, 1, 2), ("cb", 4),
    ("a2", 0, 5, 1, 1), ("a2", 1, 5, 1, 1), ("ca", 5, -1), ("ca", 5, 1), ("a2", 0, 6, 0, 1), ("a2", 1, 6, 0, 1),
    ("ca", 6, -1), ("ca", 6, 1), ("b2", 0, 0, 3), ("b2", 1, 1, 3), ("a2", 0, 7, 0, 1), ("a2", 1, 3, 1, 2),
    ("ca", 3, 2), ("a2", 0, 7, 1, 1), ("a2", 1, 7, 0, 1), ("ca", 7, -1), ("act", -1), ("a2", 1, 7, 1, 1),
    ("a2", 0, 4, 0, 2), ("ca", 4, 2), ("b2", 0, 1, 3), ("b2", 1, 0, 3), ("cb", 5), ("cb", 6), ("a2", 0, 5, 0, 2),
    ("a2", 1, 6, 1, 2), ("ca", 7, 1), ("act", 1), ("a2", 1, 5, 1, 2), ("a2", 0, 6, 0, 2), ("ca", 5, 2), ("ca", 6, 2),
    ("b2", 0, 0, 4), ("b2", 1, 1, 4), ("cb", 7), ("a2", 0, 7, 0, 2), ("a2", 1, 7, 1, 2), ("ca", 7, 2), ("act", 2),
    ("actb",),
)

SCATTER = (
    ("down", 0), ("down", 1), ("down", 2), ("down", 3), ("down", 4), ("x2", 0, 0), ("x2", 1, 0), ("down", 5),
    ("down", 6), ("yc", 0, 1), ("yc", 1, 1), ("x2", 0, 1), ("x2", 1, 1), ("down", 7), ("chk",), ("x2", 0, 2),
    ("x2", 1, 2), ("yo", 0, 2), ("yo", 1, 2), ("x2", 0, 3), ("x2", 1, 3), ("yc", 0, 2), ("yc", 1, 2), ("x2", 0, 4),
    ("x2", 1, 4), ("yo", 0, 3), ("yo", 1, 3), ("x3", 0), ("zgo",), ("x2", 0, 5), ("x2", 1, 5), ("yc", 0, 3),
    ("yc", 1, 3), ("x2", 0, 6), ("x2", 1, 6), ("x3", 1), ("zo", 0, 1), ("x2", 0, 7), ("zc", 0, 1), ("x2", 1, 7),
    ("chk2",), ("x3", 2), ("zo", 1, 1), ("zc", 1, 1), ("yend",), ("x3", 3), ("zo", 0, 2), ("x3", 4), ("zo", 1, 2),
    ("zc", 0, 2), ("chk3",), ("x3", 5), ("zc", 1, 2), ("zo", 0, 3), ("chk4",), ("zc", 0, 3), ("x3", 6), ("zo", 1, 3),
    ("x3", 7), ("zc", 1, 3), ("b2", 1), ("b2", 0), ("al1",), ("bend",), ("al2",), ("aend",),
)


def kernel(
    n_exp,
    tok_ref, ids_ref, gate_ref, dchk_ref, wg_hbm, wu_hbm, wd_hbm,
    out_ref, res_ref, alarm_ref,
    wg, wu, wd, x, p, acc_ga, acc_ua, acc_gb, acc_ub, hid, fin,
    sbuf, rbuf, bbuf, qbuf,
    xh, xf, zh, zf, yh, yf, bh, bf,
    racc, cs, cr, cf, zr, cc, es, er, gs, gr,
    w_sem, d_s, d_r, m_s, m_r,
    c_s, c_r, cc_s, cc_r, q_s, q_r, z_s, z_r, es_s, es_r, gs_s, gs_r,
):
    e = lax.axis_index("expert")
    t = lax.axis_index("tensor")
    d = lax.axis_index("dp")
    rows = x.shape[2]
    cols = x.shape[3]
    ff = wg.shape[1]
    toks = tok_ref.shape[0]
    na = rows * 3 // 5
    nb = rows - na
    A, A0, A1 = pl.ds(0, na), pl.ds(0, na // 2), pl.ds(na // 2, na // 2)
    B, B0, B1 = pl.ds(na, nb), pl.ds(na, nb // 2), pl.ds(na + nb // 2, nb // 2)

    def tz(o):
        return lax.rem(t + (o + 2 * NT), NT)

    def dx(o):
        return lax.rem(d + (o + 2 * NX), NX)

    def ex(o):
        return lax.rem(e + o, n_exp)

    zdev = ((e, tz(1), d), (e, tz(-1), d))
    xdev = ((e, t, dx(1)), (e, t, dx(-1)))

    def copy(src, dst, ssem, rsem, dev):
        return pltpu.make_async_remote_copy(
            src_ref=src, dst_ref=dst, send_sem=ssem, recv_sem=rsem,
            device_id=dev, device_id_type=MESH,
        )

    def send(src, dst, ssem, rsem, dev):
        copy(src, dst, ssem, rsem, dev).start()

    def got(dst, ssem, rsem):
        copy(dst, dst, ssem, rsem, xdev[0]).wait_recv()

    def sent(src, ssem, rsem):
        copy(src, src, ssem, rsem, xdev[0]).wait_send()

    numbers = {}
    used = []

    def number(*key):
        return numbers.setdefault(key, len(numbers))

    def post(src, dst, side, dev, *key):
        n = number(side, *key)
        used.append((src, n))
        send(src, dst, m_s.at[n], m_r.at[n], dev)

    def take(dst, side, *key):
        n = number(side, *key)
        got(dst, m_s.at[n], m_r.at[n])

    def dot_t(a, b):
        return lax.dot_general(a, b, (((1,), (1,)), ((), ())), preferred_element_type=F32)

    def turned(row):
        return jnp.transpose(jnp.broadcast_to(row, (toks, toks)))[:, 0:1]

    w_copies = [
        pltpu.make_async_copy(src.at[:, pl.ds(i * cols, cols)], dst.at[i], w_sem.at[n, i])
        for n, (src, dst) in enumerate(((wg_hbm, wg), (wu_hbm, wu), (wd_hbm, wd)))
        for i in range(NT)
    ]
    for c in w_copies:
        c.start()
    barrier = pltpu.get_barrier_semaphore()
    for o in range(1, n_exp):
        pl.semaphore_signal(barrier, inc=1, device_id=(ex(o), t, d), device_id_type=MESH)
    for o in range(1, NT):
        pl.semaphore_signal(barrier, inc=1, device_id=(e, tz(o), d), device_id_type=MESH)
    for o in range(1, NX):
        pl.semaphore_signal(barrier, inc=1, device_id=(e, t, dx(o)), device_id_type=MESH)

    ids = ids_ref[...].astype(F32)
    ids_row = [jnp.broadcast_to(ids[k : k + 1], (8, toks)) for k in range(2)]
    iota_e = lax.broadcasted_iota(jnp.int32, (8, toks), 0).astype(F32)
    count = (ids_row[0] == iota_e).astype(F32) + (ids_row[1] == iota_e).astype(F32)
    above = lax.broadcasted_iota(jnp.int32, (toks, toks), 0) < lax.broadcasted_iota(jnp.int32, (toks, toks), 1)
    before = jnp.dot(count.astype(BF16), above.astype(F32).astype(BF16), preferred_element_type=F32)
    place = jnp.where(count > 0.5, before, -1.0)
    iota_p = lax.broadcasted_iota(jnp.int32, (CAP, toks), 0).astype(F32)
    pick = jnp.concatenate(
        [(iota_p == jnp.broadcast_to(place[i : i + 1], (CAP, toks))).astype(F32) for i in range(n_exp)], axis=0
    )
    slot_rows = jnp.dot(pick.astype(BF16), tok_ref[...], preferred_element_type=F32)
    sbuf[...] = slot_rows.reshape(n_exp, CAP, cols).astype(BF16)

    pl.semaphore_wait(barrier, n_exp - 1 + NT - 1 + NX - 1)

    for o in range(1, n_exp):
        send(sbuf.at[ex(o)], rbuf.at[e], d_s.at[o - 1], d_r.at[o - 1], (ex(o), t, d))
    rbuf[e] = sbuf[e]
    acc_ga[...] = jnp.zeros_like(acc_ga)
    acc_ua[...] = jnp.zeros_like(acc_ua)
    acc_gb[...] = jnp.zeros_like(acc_gb)
    acc_ub[...] = jnp.zeros_like(acc_ub)
    for o in range(1, n_exp):
        got(rbuf.at[ex(n_exp - o)], d_s.at[o - 1], d_r.at[o - 1])
    x[t, d] = rbuf[...].astype(F32).reshape(rows, cols).astype(BF16)

    def mul_a(tp, dp):
        v = x[tp, dp, A, :]
        acc_ga[dp] += dot_t(v, wg[tp])
        acc_ua[dp] += dot_t(v, wu[tp])

    def mul_b(tp):
        v = x[tp, :, B, :].reshape(NX * nb, cols)
        acc_gb[...] += dot_t(v, wg[tp])
        acc_ub[...] += dot_t(v, wu[tp])

    def silu(g, u):
        return (g / (1.0 + jnp.exp(-g)) * u).astype(BF16)

    def act_a(dp):
        hid[dp, A, :] = silu(acc_ga[dp], acc_ua[dp])

    half_a, half_b = (A0, A1), (B0, B1)
    offs = (0, -1, 1, -2, 2, -3, 3, 4)
    sign = (-1, 1)

    def gather(kind, *key):
        if kind == "a1":
            i, h, s = key
            ref = x.at[tz(sign[i] * s), d, half_a[h]]
            take(ref, i, "a1", h, s)
            if s < 3 or (s == 3 and h == i):
                post(ref, ref, i, zdev[i], "a1", h, s + 1)
            k = 7 if s == 4 else 2 * s - 1 + i
            for ii in range(2):
                post(ref, ref, ii, xdev[ii], "a2", k, h, 1)
        elif kind == "b1":
            i, h, s = key
            ref = x.at[t, dx(sign[i] * s), half_b[h]]
            take(ref, i, "b1", h, s)
            if s == 1 and h == i:
                post(ref, ref, i, xdev[i], "b1", h, 2)
        elif kind == "b2" and not key:
            for i in range(2):
                for h in (i, 1 - i):
                    ref = x.at[t, :, half_b[h]]
                    post(ref, ref, i, zdev[i], "b2", h, 1)
        elif kind == "b2":
            i, h, s = key
            ref = x.at[tz(sign[i] * s), :, half_b[h]]
            take(ref, i, "b2", h, s)
            if s < 3 or (s == 3 and h == i):
                post(ref, ref, i, zdev[i], "b2", h, s + 1)
        elif kind == "a2":
            i, k, h, s = key
            ref = x.at[tz(offs[k]), dx(sign[i] * s), half_a[h]]
            take(ref, i, "a2", k, h, s)
            if s == 1 and h == i:
                post(ref, ref, i, xdev[i], "a2", k, h, 2)
        elif kind == "ca":
            mul_a(tz(offs[key[0]]), dx(key[1]))
        elif kind == "cb":
            mul_b(tz(offs[key[0]]))
        elif kind == "act":
            act_a(dx(key[0]))
        else:
            hb = silu(acc_gb[...], acc_ub[...])
            for n in range(NX):
                hid[n, B, :] = hb[n * nb : (n + 1) * nb]

    for i in range(2):
        for h in (i, 1 - i):
            ref = x.at[t, d, half_a[h]]
            post(ref, ref, i, zdev[i], "a1", h, 1)
    for i in range(2):
        for h in (i, 1 - i):
            ref = x.at[t, d, half_b[h]]
            post(ref, ref, i, xdev[i], "b1", h, 1)
    for i in range(2):
        for h in (i, 1 - i):
            ref = x.at[t, d, half_a[h]]
            post(ref, ref, i, xdev[i], "a2", 0, h, 1)
    for c in w_copies[: 2 * NT]:
        c.wait()
    for step in GATHER:
        gather(*step)

    for c in w_copies[2 * NT :]:
        c.wait()

    racc[...] = jnp.zeros_like(racc)

    def down(tp):
        def one(dp, carry):
            v = jnp.dot(hid[dp], wd[tp], preferred_element_type=F32).astype(BF16)
            p[tp, dp] = v
            v = v.astype(F32)
            racc[dp] += (v[:, 0:128] + v[:, 128:256]) + (v[:, 256:384] + v[:, 384:512]) if cols == 512 else v
            return carry

        lax.fori_loop(0, NX, one, 0)

    def add(tp, dp, span, *others):
        total = p[tp, dp, span, :].astype(F32)
        for o in others:
            total = total + o.astype(F32)
        p[tp, dp, span, :] = total.astype(BF16)

    far = (4, 3, -3, 2, -2, 1, -1, 0)
    side_a, side_b = ((A1, A0), (A0, A1)), ((B1, B0), (B0, B1))
    low_a, high_a = pl.ds(0, na // 2), pl.ds(na // 2, na // 2)
    low_b, high_b = pl.ds(0, nb // 2), pl.ds(nb // 2, nb // 2)
    slot_a, slot_b = ((high_a, low_a), (low_a, high_a)), ((high_b, low_b), (low_b, high_b))
    near = (1, -1)
    every = slice(None)

    def scatter(kind, *key):
        if kind == "down":
            (j,) = key
            tp = tz(far[j])
            down(tp)
            for i in range(2):
                post(p.at[tp, dx(2), side_a[i][0]], xh.at[j, i], i, xdev[i], "xh", j)
            for i in range(2):
                post(p.at[tp, dx(near[i]), side_a[i][1]], xf.at[j, i, slot_a[i][1]], i, xdev[i], "xo", j)
            if j == 0:
                for i in range(2):
                    post(p.at[tp, :, side_b[i][0]], yh.at[i], i, zdev[i], "yc", 0)
            if j in (1, 2):
                i = j - 1
                post(p.at[tp, :, side_b[i][1]], yf.at[0, i, :, slot_b[i][1]], i, zdev[i], "yo", 1)
        elif kind == "x2":
            i, j = key
            tp, dp = tz(far[j]), dx(near[i])
            take(xh.at[j, i], i, "xh", j)
            add(tp, dp, side_a[i][0], xh[j, i])
            post(p.at[tp, dp, side_a[i][0]], xf.at[j, i, slot_a[i][0]], i, xdev[i], "xf", j)
        elif kind == "x3":
            (j,) = key
            for i in range(2):
                take(xf.at[j, i, slot_a[i][1]], i, "xo", j)
                take(xf.at[j, i, slot_a[i][0]], i, "xf", j)
            add(tz(far[j]), d, A, xf[j, 0], xf[j, 1])
        elif kind in ("yc", "yo"):
            i, s = key
            n = 0 if kind == "yc" else 1
            tp = tz(near[i] * (4 - s))
            src = yh.at[i] if s == 1 else yf.at[s - 2, i, :, slot_b[i][n]]
            take(src, i, kind, s - 1)
            add(tp, every, side_b[i][n], src[...])
            post(p.at[tp, :, side_b[i][n]], yf.at[s - 1, i, :, slot_b[i][n]], i, zdev[i], kind, s)
        elif kind == "yend":
            for i in range(2):
                take(yf.at[2, i, :, slot_b[i][0]], i, "yc", 3)
                take(yf.at[2, i, :, slot_b[i][1]], i, "yo", 3)
            add(t, every, B, yf[2, 0], yf[2, 1])
            for i in range(2):
                post(p.at[t, dx(2), side_b[i][0]], bh.at[i], i, xdev[i], "bh")
            for i in range(2):
                post(p.at[t, dx(near[i]), side_b[i][1]], bf.at[i, slot_b[i][1]], i, xdev[i], "bo")
        elif kind == "b2":
            (i,) = key
            take(bh.at[i], i, "bh")
            add(t, dx(near[i]), side_b[i][0], bh[i])
            post(p.at[t, dx(near[i]), side_b[i][0]], bf.at[i, slot_b[i][0]], i, xdev[i], "bf")
        elif kind == "zgo":
            for i in range(2):
                post(p.at[tz(4), d, side_a[i][0]], zh.at[i], i, zdev[i], "zc", 0)
        elif kind in ("zc", "zo"):
            i, s = key
            n = 0 if kind == "zc" else 1
            tp = tz(near[i] * (4 - s))
            if kind == "zc" or s > 1:
                src = zh.at[i] if s == 1 else zf.at[s - 2, i, slot_a[i][n]]
                take(src, i, kind, s - 1)
                add(tp, d, side_a[i][n], src[...])
            post(p.at[tp, d, side_a[i][n]], zf.at[s - 1, i, slot_a[i][n]], i, zdev[i], kind, s)
        elif kind == "aend":
            for i in range(2):
                take(zf.at[2, i, slot_a[i][0]], i, "zc", 3)
                take(zf.at[2, i, slot_a[i][1]], i, "zo", 3)
            fin[A, :] = p[t, d, A, :].astype(F32) + zf[2, 0].astype(F32) + zf[2, 1].astype(F32)
        elif kind == "bend":
            for i in range(2):
                take(bf.at[i, slot_b[i][1]], i, "bo")
                take(bf.at[i, slot_b[i][0]], i, "bf")
            fin[B, :] = p[t, d, B, :].astype(F32) + bf[0].astype(F32) + bf[1].astype(F32)
        else:
            CHECKS[kind]()

    def chk():
        dc = jnp.broadcast_to(dchk_ref[...].astype(F32), (16, ff)).astype(BF16)
        ones = jnp.ones((8, racc.shape[2]), F32)
        for i in range(NX):
            sums = lax.dot_general(
                ones, racc[i], (((1,), (1,)), ((), ())), preferred_element_type=F32, precision=lax.Precision.HIGHEST
            )
            cs[i] = (sums - dot_t(dc, hid[i])[0:8])[0:1]
        for o in range(1, NX):
            send(cs.at[dx(o)], cr.at[o - 1], c_s.at[o - 1], c_r.at[o - 1], (e, t, dx(o)))

    def chk2():
        for o in range(1, NX):
            got(cr.at[o - 1], c_s.at[o - 1], c_r.at[o - 1])
        cf[0] = cs[d] + cr[0] + cr[1] + cr[2]
        zr[t] = cf[0]
        for o in range(1, NT):
            send(cf.at[0], zr.at[t], z_s.at[o - 1], z_r.at[o - 1], (e, tz(o), d))

    def chk3():
        for o in range(1, NT):
            got(zr.at[tz(-o)], z_s.at[o - 1], z_r.at[o - 1])
        total = zr[0]
        for i in range(1, NT):
            total = total + zr[i]
        cf[1] = total
        cc[e] = total
        for o in range(1, n_exp):
            send(cf.at[1], cc.at[e], cc_s.at[o - 1], cc_r.at[o - 1], (ex(o), t, d))

    iota_s = lax.broadcasted_iota(jnp.int32, (toks, rows), 1).astype(F32)
    route = {}

    def chk4():
        iota_l = lax.broadcasted_iota(jnp.int32, (toks, toks), 1).astype(F32)
        col = [turned(ids[k : k + 1]) for k in range(2)]
        left = [(col[k] == iota_l).astype(F32) for k in range(2)]
        below = lax.broadcasted_iota(jnp.int32, (toks, toks), 1) < lax.broadcasted_iota(jnp.int32, (toks, toks), 0)
        before_col = jnp.dot(
            below.astype(F32).astype(BF16), (left[0] + left[1]).astype(BF16), preferred_element_type=F32
        )
        pos = [jnp.sum(left[k] * before_col, axis=1, keepdims=True) for k in range(2)]
        gates = gate_ref[...].astype(F32)
        gate_sum = gates[0:1] + gates[1:2]
        weight = [turned(gates[k : k + 1] / gate_sum) for k in range(2)]
        mine = (e * CAP).astype(F32)
        for o in range(1, n_exp):
            got(cc.at[ex(n_exp - o)], cc_s.at[o - 1], cc_r.at[o - 1])
        diff = jnp.zeros((toks, 1), F32)
        for k in range(2):
            row = jnp.zeros((toks, rows), F32)
            for i in range(n_exp):
                row = row + jnp.where(col[k] == float(i), jnp.broadcast_to(cc[i], (toks, rows)), 0.0)
            picked = jnp.where(iota_s == pos[k] + mine, row, 0.0)
            diff = diff + weight[k] * jnp.sum(picked, axis=1, keepdims=True)
        residual = jnp.transpose(jnp.broadcast_to(diff, (toks, toks)))[0:1] * (1.0 / math.sqrt(D))
        res_ref[...] = residual
        score = jnp.broadcast_to(jnp.sum(residual * residual, axis=1, keepdims=True), (1, toks))
        es[...] = score
        for o in range(1, NX):
            send(es, er.at[d], es_s.at[o - 1], es_r.at[o - 1], (e, t, dx(o)))
        er[d] = score
        route["weight"] = weight
        route["slot"] = [col[k] * float(CAP) + pos[k] for k in range(2)]

    def al1():
        for o in range(1, NX):
            got(er.at[dx(-o)], es_s.at[o - 1], es_r.at[o - 1])
        score = er[0]
        for i in range(1, NX):
            score = score + er[i]
        gs[...] = score
        for o in range(1, n_exp):
            send(gs, gr.at[e], gs_s.at[o - 1], gs_r.at[o - 1], (ex(o), t, d))
        gr[e] = score

    def al2():
        for o in range(1, n_exp):
            got(gr.at[ex(n_exp - o)], gs_s.at[o - 1], gs_r.at[o - 1])
        score = gr[0]
        for i in range(1, n_exp):
            score = score + gr[i]
        alarm_ref[...] = score[0:1, 0:1] * (1.0 / (toks * n_exp * NX))

    CHECKS = {"chk": chk, "chk2": chk2, "chk3": chk3, "chk4": chk4, "al1": al1, "al2": al2}
    for step in SCATTER:
        scatter(*step)

    bbuf[...] = fin[...].reshape(n_exp, CAP, cols).astype(BF16)
    for o in range(1, n_exp):
        send(bbuf.at[ex(o)], qbuf.at[e], q_s.at[o - 1], q_r.at[o - 1], (ex(o), t, d))
    qbuf[e] = bbuf[e]
    for o in range(1, n_exp):
        got(qbuf.at[ex(n_exp - o)], q_s.at[o - 1], q_r.at[o - 1])
    back = qbuf[...].astype(F32).reshape(rows, cols).astype(BF16)
    combined = jnp.zeros((toks, cols), F32)
    for k in range(2):
        sel = (iota_s == route["slot"][k]).astype(F32).astype(BF16)
        combined = combined + route["weight"][k] * jnp.dot(sel, back, preferred_element_type=F32)
    out_ref[...] = combined

    for o in range(n_exp - 1):
        sent(sbuf.at[0], d_s.at[o], d_r.at[o])
        sent(cf.at[1], cc_s.at[o], cc_r.at[o])
        sent(bbuf.at[0], q_s.at[o], q_r.at[o])
        sent(gs, gs_s.at[o], gs_r.at[o])
    for o in range(NX - 1):
        sent(cs.at[0], c_s.at[o], c_r.at[o])
        sent(es, es_s.at[o], es_r.at[o])
    for o in range(NT - 1):
        sent(cf.at[0], z_s.at[o], z_r.at[o])
    for ref, n in used:
        sent(ref, m_s.at[n], m_r.at[n])


def body(tokens, expert_ids, gate_fixed, w_gate, w_up, w_down, down_check):
    n_exp = lax.axis_size("expert")
    toks, cols = tokens.shape
    ff = w_gate.shape[2]
    rows = n_exp * CAP
    na = rows * 3 // 5
    nb = rows - na
    dma = lambda *s: pltpu.SemaphoreType.DMA(s)
    both = lambda *s: [dma(*s), dma(*s)]
    vm = pltpu.VMEM
    scratch = [
        vm((NT, ff, cols), BF16), vm((NT, ff, cols), BF16), vm((NT, ff, cols), BF16),
        vm((NT, NX, rows, cols), BF16), vm((NT, NX, rows, cols), BF16),
        vm((NX, na, ff), F32), vm((NX, na, ff), F32), vm((NX * nb, ff), F32), vm((NX * nb, ff), F32),
        vm((NX, rows, ff), BF16), vm((rows, cols), F32),
        vm((n_exp, CAP, cols), BF16), vm((n_exp, CAP, cols), BF16),
        vm((n_exp, CAP, cols), BF16), vm((n_exp, CAP, cols), BF16),
        vm((NT, 2, na // 2, cols), BF16), vm((NT, 2, na, cols), BF16),
        vm((2, na // 2, cols), BF16), vm((3, 2, na, cols), BF16),
        vm((2, NX, nb // 2, cols), BF16), vm((3, 2, NX, nb, cols), BF16),
        vm((2, nb // 2, cols), BF16), vm((2, nb, cols), BF16),
        vm((NX, rows, min(cols, 128)), F32),
        vm((NX, 1, rows), F32), vm((NX - 1, 1, rows), F32), vm((2, 1, rows), F32), vm((NT, 1, rows), F32),
        vm((n_exp, 1, rows), F32), vm((1, toks), F32), vm((NX, 1, toks), F32),
        vm((1, toks), F32), vm((n_exp, 1, toks), F32),
        dma(3, NT), *both(n_exp - 1), *both(MESSAGES),
        *both(NX - 1), *both(n_exp - 1), *both(n_exp - 1), *both(NT - 1), *both(NX - 1), *both(n_exp - 1),
    ]
    vmem = pl.BlockSpec(memory_space=pltpu.VMEM)
    hbm = pl.BlockSpec(memory_space=pl.ANY)
    mix, residual, alarm = pl.pallas_call(
        functools.partial(kernel, n_exp),
        out_shape=(
            jax.ShapeDtypeStruct((toks, cols), F32),
            jax.ShapeDtypeStruct((1, toks), F32),
            jax.ShapeDtypeStruct((1, 1), F32),
        ),
        in_specs=[vmem, vmem, vmem, vmem, hbm, hbm, hbm],
        out_specs=(vmem, vmem, vmem),
        scratch_shapes=scratch,
        compiler_params=pltpu.CompilerParams(
            collective_id=0, has_side_effects=True, vmem_limit_bytes=66_000_000
        ),
    )(
        tokens, expert_ids.T, gate_fixed.T, down_check,
        w_gate[0].T, w_up[0].T, w_down[0],
    )
    return mix, residual.reshape(toks), alarm.reshape(())


def solution(mesh):
    return jax.shard_map(
        body,
        mesh=mesh,
        in_specs=(
            P(("expert", "dp"), "tensor"),
            P(("expert", "dp"), None),
            P(("expert", "dp"), None),
            P("expert", None, ("tensor", "dp")),
            P("expert", None, ("tensor", "dp")),
            P("expert", ("tensor", "dp"), None),
            P("expert", ("tensor", "dp")),
        ),
        out_specs=(P(("expert", "dp"), "tensor"), P(("expert", "dp")), P()),
        check_vma=False,
    )
```

time: 360 us -> 154 us (0.43)
  waiting for transfers between devices: 243 us -> 0 us
  Pallas kernels: 0 us -> 149 us
  matrix products: 27.2 us -> 0 us
  starting transfers between devices: 25.4 us -> 0 us
  local copies, waits for them, and re-layouts: 26.6 us -> 2.8 us
  blocking collectives: 13.7 us -> 0 us
  between operations: 15.8 us -> 2.32 us
  other arithmetic: 8.17 us -> 0 us
    pallas_call x0 -> x1, Pallas kernels: none -> 149 us  [body(): pl.pallas_call(functools.partial(kernel, n_exp), out_shape=(jax.ShapeDtyp...]
    reduce_scatter x2 -> x0, waiting for transfers between devices: 119 us -> none  [scatter_axes(): nearer = lax.psum_scatter(x, axes[0], scatter_dimension=dim, tiled=True)]
    all_gather x1 -> x0, waiting for transfers between devices: 94.5 us -> none  [body(): lax.all_gather(received[None], ('tensor', 'dp'), axis=0, tiled=True)]
    all_to_all x4 -> x0, waiting for transfers between devices: 29 us -> none  [the longest x3 21.4 us: copy_for_each(): return lax.all_to_all(copies, axis, split_axis=0, concat_axis=0, tiled=True)]
    dot_general x4 -> x0, matrix products: 27.2 us -> none  [the longest x1 11.3 us: body(): jnp.einsum('trc,tcf->rf', block_rows, gate_weights, preferred_element_typ...]
    all_to_all x4 -> x0, starting transfers between devices: 25.1 us -> none  [the longest x3 18.9 us: copy_for_each(): return lax.all_to_all(copies, axis, split_axis=0, concat_axis=0, tiled=True)]
    all_to_all x1 -> x0, blocking collectives: 13.7 us -> none  [body(): lax.all_to_all(send_buffer, 'expert', split_axis=0, concat_axis=0, tiled=...]
    unnamed x22 -> x2, local copies, waits for them, and re-layouts: 16.1 us -> 2.8 us
  transfers between devices with their start and end apart: 7 -> 0, of which waited for: 7 -> 0; matrix products, arithmetic and copies ran while one was open for 6% -> 0% of each run, Pallas kernels for 0% -> 0%
where the time goes in v2:
time: 154 us
  Pallas kernels  149 us (97%)
  local copies, waits for them, and re-layouts  2.8 us (2%)
  between operations  2.32 us (2%)
    pallas_call x1, Pallas kernels, body(): pl.pallas_call(functools.partial(kernel, n_exp), out_shape=(jax.ShapeDtyp...  149 us

profile of v2, /device:TPU:1, one launch (start us, length us, event | category | flops | bytes accessed | tf_op | source)
XLA Modules:
  0.0 153.6 jit_solution(9130310704404251782)
XLA Ops:
  0.6 148.5 %shard_map.94 = (f32[128,512]{1,0:T(8,128)}, f32[1,128]{1,0:T(1,128)}, f32[1,1]{1,0:T(1,128)}) custom-call(bf16[128,512]{1,0:T(8,128)(2,1)} %tok_ref.1, s32[2,128]{1,0:T(2,128)} %bitcast.14, s32[2,128]{1,0:T(2,128)} %bitcast.15, bf16[1,448]{1,0:T(2,128)(2,1)} %dchk_ref.1, bf16[448,4096]{1,0:T(8,128)(2,1)} %bitcast.11, bf16[448,4096]{1,0:T(8,128)(2,1)} %bitcast.12, ...), custom_call_target="tpu_custom_call" | custom-call | tf_op jit(solution)/shard_map/pallas_call | solution.py:498
  149.1 1.7 %copy.13 = f32[128,512]{1,0:T(8,128)} copy(f32[128,512]{1,0:T(8,128)} %get-tuple-element.12) | data formatting | bytes 524288
  150.8 1.1 copy.14

commit v3 on v2

--- a/solution.py
+++ b/solution.py
@@ -18,38 +18,41 @@
 BF16 = jnp.bfloat16
 
 GATHER = (
-    ("ca", 0, 0), ("b1", 0, 0, 1), ("b1", 1, 1, 1), ("a1", 0, 0, 1), ("a1", 1, 1, 1), ("b1", 0, 1, 1),
-    ("b1", 1, 0, 1), ("a1", 0, 1, 1), ("a1", 1, 0, 1), ("ca", 1, 0), ("ca", 2, 0), ("a2", 0, 0, 0, 1),
-    ("a2", 1, 0, 1, 1), ("a1", 0, 0, 2), ("a1", 1, 1, 2), ("a2", 0, 0, 1, 1), ("a2", 1, 0, 0, 1), ("ca", 0, -1),
-    ("ca", 0, 1), ("b1", 0, 0, 2), ("b1", 1, 1, 2), ("b2",), ("a1", 0, 1, 2), ("a1", 1, 0, 2), ("cb", 0),
-    ("ca", 3, 0), ("ca", 4, 0), ("a1", 0, 0, 3), ("a1", 1, 1, 3), ("a2", 0, 1, 0, 1), ("a2", 1, 1, 0, 1),
-    ("a2", 0, 2, 1, 1), ("a2", 1, 2, 1, 1), ("a2", 0, 1, 1, 1), ("a2", 1, 1, 1, 1), ("ca", 1, -1), ("ca", 1, 1),
-    ("b2", 0, 0, 1), ("b2", 1, 1, 1), ("a2", 0, 2, 0, 1), ("a2", 1, 2, 0, 1), ("ca", 2, -1), ("ca", 2, 1),
-    ("a2", 0, 0, 0, 2), ("a2", 1, 0, 1, 2), ("ca", 0, 2), ("a2", 0, 3, 0, 1), ("a2", 1, 3, 0, 1), ("b2", 0, 1, 1),
-    ("b2", 1, 0, 1), ("cb", 1), ("a2", 0, 4, 1, 1), ("a2", 1, 4, 1, 1), ("cb", 2), ("a1", 0, 1, 3), ("a1", 1, 0, 3),
-    ("ca", 5, 0), ("a2", 0, 3, 1, 1), ("a2", 1, 3, 1, 1), ("ca", 3, -1), ("ca", 3, 1), ("a1", 0, 0, 4),
-    ("a1", 1, 1, 4), ("ca", 6, 0), ("ca", 7, 0), ("a2", 0, 4, 0, 1), ("a2", 1, 4, 0, 1), ("ca", 4, -1), ("ca", 4, 1),
-    ("act", 0), ("a2", 0, 5, 0, 1), ("a2", 1, 5, 0, 1), ("a2", 0, 6, 1, 1), ("a2", 1, 6, 1, 1), ("b2", 0, 0, 2),
-    ("b2", 1, 1, 2), ("a2", 0, 1, 0, 2), ("a2", 1, 2, 1, 2), ("a2", 1, 1, 1, 2), ("a2", 0, 2, 0, 2), ("ca", 1, 2),
-    ("ca", 2, 2), ("b2", 0, 1, 2), ("b2", 1, 0, 2), ("cb", 3), ("a2", 0, 3, 0, 2), ("a2", 1, 4, 1, 2), ("cb", 4),
-    ("a2", 0, 5, 1, 1), ("a2", 1, 5, 1, 1), ("ca", 5, -1), ("ca", 5, 1), ("a2", 0, 6, 0, 1), ("a2", 1, 6, 0, 1),
-    ("ca", 6, -1), ("ca", 6, 1), ("b2", 0, 0, 3), ("b2", 1, 1, 3), ("a2", 0, 7, 0, 1), ("a2", 1, 3, 1, 2),
-    ("ca", 3, 2), ("a2", 0, 7, 1, 1), ("a2", 1, 7, 0, 1), ("ca", 7, -1), ("act", -1), ("a2", 1, 7, 1, 1),
-    ("a2", 0, 4, 0, 2), ("ca", 4, 2), ("b2", 0, 1, 3), ("b2", 1, 0, 3), ("cb", 5), ("cb", 6), ("a2", 0, 5, 0, 2),
-    ("a2", 1, 6, 1, 2), ("ca", 7, 1), ("act", 1), ("a2", 1, 5, 1, 2), ("a2", 0, 6, 0, 2), ("ca", 5, 2), ("ca", 6, 2),
-    ("b2", 0, 0, 4), ("b2", 1, 1, 4), ("cb", 7), ("a2", 0, 7, 0, 2), ("a2", 1, 7, 1, 2), ("ca", 7, 2), ("act", 2),
-    ("actb",),
+    ("a2go",), ("b1go",), ("a1", 1, 1, 1), ("s2", 1, 1, 1), ("a1", 0, 0, 1), ("a1", 0, 1, 1), ("a1", 1, 0, 1),
+    ("b1", 1, 1, 1), ("b1", 0, 0, 1), ("a1", 1, 1, 2), ("a1", 0, 0, 2), ("s2", 1, 0, 1), ("a1", 1, 0, 2),
+    ("a1", 0, 1, 2), ("s2", 0, 1, 2), ("b1", 1, 0, 1), ("b1", 0, 1, 1), ("b1", 1, 1, 2), ("b1", 0, 0, 2), ("b2",),
+    ("a1", 0, 0, 3), ("a1", 1, 1, 3), ("ca", 4, 0), ("s2", 1, 1, 3), ("a2", 1, 0, 1, 1), ("ca", 0, 0),
+    ("a1", 1, 0, 3), ("s2", 1, 0, 3), ("cb", 0), ("s2", 1, 0, 2), ("s2", 1, 1, 2), ("b2", 0, 0, 1), ("b2", 1, 1, 1),
+    ("ca", 2, 0), ("a2", 0, 2, 1, 1), ("a2", 0, 0, 0, 1), ("a1", 0, 1, 3), ("a2", 1, 4, 0, 1), ("a2", 1, 2, 0, 1),
+    ("s2", 0, 1, 3), ("a2", 1, 6, 1, 1), ("ca", 6, 0), ("a2", 1, 0, 1, 2), ("a2", 0, 6, 0, 1), ("s2", 0, 0, 3),
+    ("b2", 1, 0, 1), ("a2", 1, 4, 1, 1), ("a1", 1, 1, 4), ("s2", 0, 0, 1), ("s2", 0, 0, 2), ("s2", 1, 1, 4),
+    ("a1", 0, 0, 4), ("a2", 1, 6, 0, 1), ("a2", 0, 0, 0, 2), ("s2", 0, 1, 1), ("b2", 0, 1, 1), ("ca", 3, 0),
+    ("a2", 1, 0, 0, 1), ("a2", 0, 0, 1, 1), ("ca", 0, -1), ("ca", 1, 0), ("ca", 5, 0), ("a2", 0, 3, 1, 1),
+    ("ca", 4, 1), ("a2", 0, 4, 0, 1), ("s2", 0, 0, 4), ("ca", 7, 0), ("act", 0), ("a2", 0, 2, 0, 1),
+    ("a2", 1, 2, 1, 1), ("a2", 1, 3, 1, 1), ("ca", 0, 2), ("a2", 0, 4, 1, 1), ("b2", 0, 0, 2), ("a2", 0, 6, 0, 2),
+    ("a2", 0, 6, 1, 1), ("a2", 0, 5, 1, 1), ("ca", 4, -1), ("cb", 1), ("ca", 6, 1), ("b2", 1, 1, 2),
+    ("a2", 1, 5, 1, 1), ("ca", 6, -1), ("a2", 1, 6, 1, 2), ("a2", 1, 5, 0, 1), ("ca", 0, 1), ("a2", 1, 1, 0, 1),
+    ("cb", 2), ("b2", 0, 1, 2), ("ca", 6, 2), ("b2", 1, 0, 2), ("cb", 4), ("ca", 2, 1), ("ca", 2, -1), ("cb", 3),
+    ("a2", 0, 5, 0, 1), ("a2", 1, 3, 0, 1), ("ca", 3, 1), ("a2", 0, 3, 0, 1), ("b2", 0, 0, 3), ("b2", 1, 1, 3),
+    ("a2", 1, 4, 1, 2), ("a2", 1, 1, 1, 1), ("a2", 0, 4, 0, 2), ("ca", 3, -1), ("ca", 4, 2), ("a2", 1, 7, 1, 1),
+    ("a2", 0, 1, 0, 1), ("a2", 0, 1, 1, 1), ("ca", 1, -1), ("ca", 1, 1), ("ca", 5, -1), ("ca", 5, 1),
+    ("a2", 1, 7, 0, 1), ("ca", 7, 1), ("act", 1), ("a2", 0, 7, 0, 1), ("a2", 0, 7, 1, 1), ("ca", 7, -1),
+    ("a2", 1, 2, 1, 2), ("a2", 0, 2, 0, 2), ("b2", 1, 0, 3), ("cb", 6), ("a2", 0, 5, 0, 2), ("b2", 0, 1, 3),
+    ("cb", 5), ("a2", 1, 5, 1, 2), ("ca", 5, 2), ("act", -1), ("ca", 2, 2), ("a2", 1, 3, 1, 2), ("a2", 0, 3, 0, 2),
+    ("ca", 3, 2), ("a2", 0, 1, 0, 2), ("a2", 1, 1, 1, 2), ("ca", 1, 2), ("b2", 1, 1, 4), ("b2", 0, 0, 4), ("cb", 7),
+    ("a2", 0, 7, 0, 2), ("a2", 1, 7, 1, 2), ("ca", 7, 2), ("act", 2), ("actb",),
 )
 
 SCATTER = (
-    ("down", 0), ("down", 1), ("down", 2), ("down", 3), ("down", 4), ("x2", 0, 0), ("x2", 1, 0), ("down", 5),
-    ("down", 6), ("yc", 0, 1), ("yc", 1, 1), ("x2", 0, 1), ("x2", 1, 1), ("down", 7), ("chk",), ("x2", 0, 2),
-    ("x2", 1, 2), ("yo", 0, 2), ("yo", 1, 2), ("x2", 0, 3), ("x2", 1, 3), ("yc", 0, 2), ("yc", 1, 2), ("x2", 0, 4),
-    ("x2", 1, 4), ("yo", 0, 3), ("yo", 1, 3), ("x3", 0), ("zgo",), ("x2", 0, 5), ("x2", 1, 5), ("yc", 0, 3),
-    ("yc", 1, 3), ("x2", 0, 6), ("x2", 1, 6), ("x3", 1), ("zo", 0, 1), ("x2", 0, 7), ("zc", 0, 1), ("x2", 1, 7),
-    ("chk2",), ("x3", 2), ("zo", 1, 1), ("zc", 1, 1), ("yend",), ("x3", 3), ("zo", 0, 2), ("x3", 4), ("zo", 1, 2),
-    ("zc", 0, 2), ("chk3",), ("x3", 5), ("zc", 1, 2), ("zo", 0, 3), ("chk4",), ("zc", 0, 3), ("x3", 6), ("zo", 1, 3),
-    ("x3", 7), ("zc", 1, 3), ("b2", 1), ("b2", 0), ("al1",), ("bend",), ("al2",), ("aend",),
+    ("down", 0), ("down", 1), ("down", 2), ("down", 3), ("down", 4), ("xo", 1), ("yc", 0, 1), ("x2", 1, 0),
+    ("x2", 0, 0), ("xo", 0), ("yc", 1, 1), ("x2", 0, 1), ("x2", 1, 1), ("x2", 1, 3), ("down", 5), ("down", 6),
+    ("xo", 2), ("yo", 1, 2), ("down", 7), ("x2", 1, 2), ("chk",), ("xo", 3), ("yo", 0, 2), ("xo", 5), ("x3", 0),
+    ("zgo",), ("x3", 1), ("x2", 0, 3), ("x2", 0, 4), ("yc", 0, 2), ("yc", 1, 2), ("x2", 0, 2), ("xo", 4),
+    ("yo", 0, 3), ("xo", 6), ("yo", 1, 3), ("chk2",), ("x2", 1, 4), ("yc", 1, 3), ("x2", 0, 5), ("x2", 1, 6),
+    ("yc", 0, 3), ("x2", 1, 5), ("chk3",), ("x2", 0, 6), ("x3", 2), ("zo", 1, 1), ("zc", 0, 1), ("chk4",),
+    ("zc", 1, 1), ("zo", 0, 1), ("yend",), ("x3", 4), ("xo", 7), ("x3", 3), ("zo", 1, 2), ("zc", 0, 2), ("zc", 1, 2),
+    ("zo", 0, 2), ("x3", 6), ("al1",), ("x3", 5), ("b2", 1), ("b2", 0), ("zc", 0, 3), ("x2", 0, 7), ("zo", 1, 3),
+    ("x2", 1, 7), ("al2",), ("zc", 1, 3), ("zo", 0, 3), ("bend",), ("x3", 7), ("aend",),
 )
 
 
@@ -85,6 +88,19 @@
     def ex(o):
         return lax.rem(e + o, n_exp)
 
+    y, core = lax.div(e, 2), lax.rem(e, 2)
+    ny = n_exp // 2
+    steps = [0, 1, ny - 1] + list(range(2, ny - 1))
+
+    def source(j):
+        return 2 * lax.rem(y + steps[j // 2], ny) + lax.rem(core + j % 2, 2)
+
+    def expert_at(j):
+        return 2 * lax.rem(y + ny - steps[j // 2], ny) + lax.rem(core + j % 2, 2)
+
+    until_a = -(-na // CAP)
+    from_b = na // CAP
+
     zdev = ((e, tz(1), d), (e, tz(-1), d))
     xdev = ((e, t, dx(1)), (e, t, dx(-1)))
 
@@ -155,16 +171,16 @@
 
     pl.semaphore_wait(barrier, n_exp - 1 + NT - 1 + NX - 1)
 
-    for o in range(1, n_exp):
-        send(sbuf.at[ex(o)], rbuf.at[e], d_s.at[o - 1], d_r.at[o - 1], (ex(o), t, d))
-    rbuf[e] = sbuf[e]
+    for j in reversed(range(1, n_exp)):
+        send(sbuf.at[expert_at(j)], rbuf.at[j], d_s.at[j - 1], d_r.at[j - 1], (expert_at(j), t, d))
+    rbuf[0] = sbuf[e]
     acc_ga[...] = jnp.zeros_like(acc_ga)
     acc_ua[...] = jnp.zeros_like(acc_ua)
     acc_gb[...] = jnp.zeros_like(acc_gb)
     acc_ub[...] = jnp.zeros_like(acc_ub)
-    for o in range(1, n_exp):
-        got(rbuf.at[ex(n_exp - o)], d_s.at[o - 1], d_r.at[o - 1])
-    x[t, d] = rbuf[...].astype(F32).reshape(rows, cols).astype(BF16)
+    for j in range(1, until_a):
+        got(rbuf.at[j], d_s.at[j - 1], d_r.at[j - 1])
+    x[t, d, A, :] = rbuf[0:until_a].astype(F32).reshape(until_a * CAP, cols)[0:na].astype(BF16)
 
     def mul_a(tp, dp):
         v = x[tp, dp, A, :]
@@ -193,9 +209,26 @@
             take(ref, i, "a1", h, s)
             if s < 3 or (s == 3 and h == i):
                 post(ref, ref, i, zdev[i], "a1", h, s + 1)
+        elif kind == "s2":
+            i, h, s = key
+            ref = x.at[tz(sign[i] * s), d, half_a[h]]
             k = 7 if s == 4 else 2 * s - 1 + i
             for ii in range(2):
                 post(ref, ref, ii, xdev[ii], "a2", k, h, 1)
+        elif kind == "a2go":
+            for i in range(2):
+                for h in (i, 1 - i):
+                    ref = x.at[t, d, half_a[h]]
+                    post(ref, ref, i, xdev[i], "a2", 0, h, 1)
+        elif kind == "b1go":
+            for j in range(until_a, n_exp):
+                got(rbuf.at[j], d_s.at[j - 1], d_r.at[j - 1])
+            late = rbuf[from_b:n_exp].astype(F32).reshape((n_exp - from_b) * CAP, cols)
+            x[t, d, B, :] = late[na - from_b * CAP :].astype(BF16)
+            for i in range(2):
+                for h in (i, 1 - i):
+                    ref = x.at[t, d, half_b[h]]
+                    post(ref, ref, i, xdev[i], "b1", h, 1)
         elif kind == "b1":
             i, h, s = key
             ref = x.at[t, dx(sign[i] * s), half_b[h]]
@@ -234,14 +267,6 @@
         for h in (i, 1 - i):
             ref = x.at[t, d, half_a[h]]
             post(ref, ref, i, zdev[i], "a1", h, 1)
-    for i in range(2):
-        for h in (i, 1 - i):
-            ref = x.at[t, d, half_b[h]]
-            post(ref, ref, i, xdev[i], "b1", h, 1)
-    for i in range(2):
-        for h in (i, 1 - i):
-            ref = x.at[t, d, half_a[h]]
-            post(ref, ref, i, xdev[i], "a2", 0, h, 1)
     for c in w_copies[: 2 * NT]:
         c.wait()
     for step in GATHER:
@@ -276,6 +301,16 @@
     near = (1, -1)
     every = slice(None)
 
+    def hand_back(first, last):
+        if first == last:
+            return
+        done = fin[pl.ds(first * CAP, (last - first) * CAP), :]
+        bbuf[first:last] = done.reshape(last - first, CAP, cols).astype(BF16)
+        for j in reversed(range(max(first, 1), last)):
+            send(bbuf.at[j], qbuf.at[e], q_s.at[j - 1], q_r.at[j - 1], (source(j), t, d))
+        if first == 0:
+            qbuf[e] = bbuf[0]
+
     def scatter(kind, *key):
         if kind == "down":
             (j,) = key
@@ -283,14 +318,17 @@
             down(tp)
             for i in range(2):
                 post(p.at[tp, dx(2), side_a[i][0]], xh.at[j, i], i, xdev[i], "xh", j)
-            for i in range(2):
-                post(p.at[tp, dx(near[i]), side_a[i][1]], xf.at[j, i, slot_a[i][1]], i, xdev[i], "xo", j)
             if j == 0:
                 for i in range(2):
                     post(p.at[tp, :, side_b[i][0]], yh.at[i], i, zdev[i], "yc", 0)
             if j in (1, 2):
                 i = j - 1
                 post(p.at[tp, :, side_b[i][1]], yf.at[0, i, :, slot_b[i][1]], i, zdev[i], "yo", 1)
+        elif kind == "xo":
+            (j,) = key
+            for i in range(2):
+                src = p.at[tz(far[j]), dx(near[i]), side_a[i][1]]
+                post(src, xf.at[j, i, slot_a[i][1]], i, xdev[i], "xo", j)
         elif kind == "x2":
             i, j = key
             tp, dp = tz(far[j]), dx(near[i])
@@ -342,11 +380,13 @@
                 take(zf.at[2, i, slot_a[i][0]], i, "zc", 3)
                 take(zf.at[2, i, slot_a[i][1]], i, "zo", 3)
             fin[A, :] = p[t, d, A, :].astype(F32) + zf[2, 0].astype(F32) + zf[2, 1].astype(F32)
+            hand_back(0, until_a)
         elif kind == "bend":
             for i in range(2):
                 take(bf.at[i, slot_b[i][1]], i, "bo")
                 take(bf.at[i, slot_b[i][0]], i, "bf")
             fin[B, :] = p[t, d, B, :].astype(F32) + bf[0].astype(F32) + bf[1].astype(F32)
+            hand_back(until_a, n_exp)
         else:
             CHECKS[kind]()
 
@@ -376,9 +416,9 @@
         for i in range(1, NT):
             total = total + zr[i]
         cf[1] = total
-        cc[e] = total
-        for o in range(1, n_exp):
-            send(cf.at[1], cc.at[e], cc_s.at[o - 1], cc_r.at[o - 1], (ex(o), t, d))
+        cc[0] = total
+        for j in range(1, n_exp):
+            send(cf.at[1], cc.at[j], cc_s.at[j - 1], cc_r.at[j - 1], (source(j), t, d))
 
     iota_s = lax.broadcasted_iota(jnp.int32, (toks, rows), 1).astype(F32)
     route = {}
@@ -395,15 +435,17 @@
         gates = gate_ref[...].astype(F32)
         gate_sum = gates[0:1] + gates[1:2]
         weight = [turned(gates[k : k + 1] / gate_sum) for k in range(2)]
-        mine = (e * CAP).astype(F32)
-        for o in range(1, n_exp):
-            got(cc.at[ex(n_exp - o)], cc_s.at[o - 1], cc_r.at[o - 1])
+        for j in range(1, n_exp):
+            got(cc.at[j], cc_s.at[j - 1], cc_r.at[j - 1])
         diff = jnp.zeros((toks, 1), F32)
         for k in range(2):
             row = jnp.zeros((toks, rows), F32)
-            for i in range(n_exp):
-                row = row + jnp.where(col[k] == float(i), jnp.broadcast_to(cc[i], (toks, rows)), 0.0)
-            picked = jnp.where(iota_s == pos[k] + mine, row, 0.0)
+            place = pos[k]
+            for j in range(n_exp):
+                here = col[k] == expert_at(j).astype(F32)
+                row = row + jnp.where(here, jnp.broadcast_to(cc[j], (toks, rows)), 0.0)
+                place = place + jnp.where(here, float(CAP * j), 0.0)
+            picked = jnp.where(iota_s == place, row, 0.0)
             diff = diff + weight[k] * jnp.sum(picked, axis=1, keepdims=True)
         residual = jnp.transpose(jnp.broadcast_to(diff, (toks, toks)))[0:1] * (1.0 / math.sqrt(D))
         res_ref[...] = residual
@@ -438,12 +480,8 @@
     for step in SCATTER:
         scatter(*step)
 
-    bbuf[...] = fin[...].reshape(n_exp, CAP, cols).astype(BF16)
-    for o in range(1, n_exp):
-        send(bbuf.at[ex(o)], qbuf.at[e], q_s.at[o - 1], q_r.at[o - 1], (ex(o), t, d))
-    qbuf[e] = bbuf[e]
-    for o in range(1, n_exp):
-        got(qbuf.at[ex(n_exp - o)], q_s.at[o - 1], q_r.at[o - 1])
+    for j in range(1, n_exp):
+        got(qbuf.at[expert_at(j)], q_s.at[j - 1], q_r.at[j - 1])
     back = qbuf[...].astype(F32).reshape(rows, cols).astype(BF16)
     combined = jnp.zeros((toks, cols), F32)
     for k in range(2):

time: 154 us -> 149 us (0.968)
  Pallas kernels: 149 us -> 144 us
    pallas_call x1, Pallas kernels: 149 us -> 144 us  [body(): pl.pallas_call(functools.partial(kernel, n_exp), out_shape=(jax.ShapeDtyp...]
where the time goes in v3:
time: 149 us
  Pallas kernels  144 us (97%)
  local copies, waits for them, and re-layouts  2.8 us (2%)
  between operations  2.32 us (2%)
    pallas_call x1, Pallas kernels, body(): pl.pallas_call(functools.partial(kernel, n_exp), out_shape=(jax.ShapeDtyp...  144 us

profile of v3, /device:TPU:1, one launch (start us, length us, event | category | flops | bytes accessed | tf_op | source)
XLA Modules:
  0.0 148.9 jit_solution(4960174687055559971)
XLA Ops:
  0.6 143.7 %shard_map.94 = (f32[128,512]{1,0:T(8,128)}, f32[1,128]{1,0:T(1,128)}, f32[1,1]{1,0:T(1,128)}) custom-call(bf16[128,512]{1,0:T(8,128)(2,1)} %tok_ref.1, s32[2,128]{1,0:T(2,128)} %bitcast.14, s32[2,128]{1,0:T(2,128)} %bitcast.15, bf16[1,448]{1,0:T(2,128)(2,1)} %dchk_ref.1, bf16[448,4096]{1,0:T(8,128)(2,1)} %bitcast.11, bf16[448,4096]{1,0:T(8,128)(2,1)} %bitcast.12, ...), custom_call_target="tpu_custom_call" | custom-call | tf_op jit(solution)/shard_map/pallas_call | solution.py:536
  144.4 1.7 %copy.13 = f32[128,512]{1,0:T(8,128)} copy(f32[128,512]{1,0:T(8,128)} %get-tuple-element.12) | data formatting | bytes 524288
  146.0 1.1 copy.14

commit v4 on v3

--- a/solution.py
+++ b/solution.py
@@ -18,50 +18,50 @@
 BF16 = jnp.bfloat16
 
 GATHER = (
-    ("a2go",), ("b1go",), ("a1", 1, 1, 1), ("s2", 1, 1, 1), ("a1", 0, 0, 1), ("a1", 0, 1, 1), ("a1", 1, 0, 1),
-    ("b1", 1, 1, 1), ("b1", 0, 0, 1), ("a1", 1, 1, 2), ("a1", 0, 0, 2), ("s2", 1, 0, 1), ("a1", 1, 0, 2),
-    ("a1", 0, 1, 2), ("s2", 0, 1, 2), ("b1", 1, 0, 1), ("b1", 0, 1, 1), ("b1", 1, 1, 2), ("b1", 0, 0, 2), ("b2",),
-    ("a1", 0, 0, 3), ("a1", 1, 1, 3), ("ca", 4, 0), ("s2", 1, 1, 3), ("a2", 1, 0, 1, 1), ("ca", 0, 0),
-    ("a1", 1, 0, 3), ("s2", 1, 0, 3), ("cb", 0), ("s2", 1, 0, 2), ("s2", 1, 1, 2), ("b2", 0, 0, 1), ("b2", 1, 1, 1),
-    ("ca", 2, 0), ("a2", 0, 2, 1, 1), ("a2", 0, 0, 0, 1), ("a1", 0, 1, 3), ("a2", 1, 4, 0, 1), ("a2", 1, 2, 0, 1),
-    ("s2", 0, 1, 3), ("a2", 1, 6, 1, 1), ("ca", 6, 0), ("a2", 1, 0, 1, 2), ("a2", 0, 6, 0, 1), ("s2", 0, 0, 3),
-    ("b2", 1, 0, 1), ("a2", 1, 4, 1, 1), ("a1", 1, 1, 4), ("s2", 0, 0, 1), ("s2", 0, 0, 2), ("s2", 1, 1, 4),
-    ("a1", 0, 0, 4), ("a2", 1, 6, 0, 1), ("a2", 0, 0, 0, 2), ("s2", 0, 1, 1), ("b2", 0, 1, 1), ("ca", 3, 0),
-    ("a2", 1, 0, 0, 1), ("a2", 0, 0, 1, 1), ("ca", 0, -1), ("ca", 1, 0), ("ca", 5, 0), ("a2", 0, 3, 1, 1),
-    ("ca", 4, 1), ("a2", 0, 4, 0, 1), ("s2", 0, 0, 4), ("ca", 7, 0), ("act", 0), ("a2", 0, 2, 0, 1),
-    ("a2", 1, 2, 1, 1), ("a2", 1, 3, 1, 1), ("ca", 0, 2), ("a2", 0, 4, 1, 1), ("b2", 0, 0, 2), ("a2", 0, 6, 0, 2),
-    ("a2", 0, 6, 1, 1), ("a2", 0, 5, 1, 1), ("ca", 4, -1), ("cb", 1), ("ca", 6, 1), ("b2", 1, 1, 2),
-    ("a2", 1, 5, 1, 1), ("ca", 6, -1), ("a2", 1, 6, 1, 2), ("a2", 1, 5, 0, 1), ("ca", 0, 1), ("a2", 1, 1, 0, 1),
-    ("cb", 2), ("b2", 0, 1, 2), ("ca", 6, 2), ("b2", 1, 0, 2), ("cb", 4), ("ca", 2, 1), ("ca", 2, -1), ("cb", 3),
-    ("a2", 0, 5, 0, 1), ("a2", 1, 3, 0, 1), ("ca", 3, 1), ("a2", 0, 3, 0, 1), ("b2", 0, 0, 3), ("b2", 1, 1, 3),
-    ("a2", 1, 4, 1, 2), ("a2", 1, 1, 1, 1), ("a2", 0, 4, 0, 2), ("ca", 3, -1), ("ca", 4, 2), ("a2", 1, 7, 1, 1),
-    ("a2", 0, 1, 0, 1), ("a2", 0, 1, 1, 1), ("ca", 1, -1), ("ca", 1, 1), ("ca", 5, -1), ("ca", 5, 1),
-    ("a2", 1, 7, 0, 1), ("ca", 7, 1), ("act", 1), ("a2", 0, 7, 0, 1), ("a2", 0, 7, 1, 1), ("ca", 7, -1),
-    ("a2", 1, 2, 1, 2), ("a2", 0, 2, 0, 2), ("b2", 1, 0, 3), ("cb", 6), ("a2", 0, 5, 0, 2), ("b2", 0, 1, 3),
-    ("cb", 5), ("a2", 1, 5, 1, 2), ("ca", 5, 2), ("act", -1), ("ca", 2, 2), ("a2", 1, 3, 1, 2), ("a2", 0, 3, 0, 2),
-    ("ca", 3, 2), ("a2", 0, 1, 0, 2), ("a2", 1, 1, 1, 2), ("ca", 1, 2), ("b2", 1, 1, 4), ("b2", 0, 0, 4), ("cb", 7),
-    ("a2", 0, 7, 0, 2), ("a2", 1, 7, 1, 2), ("ca", 7, 2), ("act", 2), ("actb",),
+    ("a2go",), ("b1go",), ("a1", 1, 1, 1), ("a1", 0, 0, 1), ("s2", 0, 0, 1), ("a1", 1, 0, 1), ("a1", 0, 1, 1),
+    ("a2", 1, 0, 0, 1), ("b1", 1, 1, 1), ("b1", 0, 0, 1), ("a1", 1, 1, 2), ("a1", 0, 0, 2), ("b1", 1, 0, 1),
+    ("s2", 1, 1, 2), ("a1", 1, 0, 2), ("a1", 0, 1, 2), ("a2", 1, 0, 1, 1), ("s2", 1, 0, 2), ("ca", 4, 0),
+    ("s2", 0, 1, 1), ("b1", 0, 1, 1), ("b1", 0, 0, 2), ("b1", 1, 1, 2), ("b2",), ("a1", 0, 1, 3), ("s2", 0, 0, 2),
+    ("ca", 1, 0), ("ca", 0, 0), ("s2", 1, 1, 1), ("a2", 1, 1, 1, 1), ("s2", 1, 0, 1), ("cb", 0), ("a1", 0, 0, 3),
+    ("s2", 0, 0, 3), ("s2", 0, 1, 2), ("a2", 1, 3, 0, 1), ("b2", 0, 0, 1), ("a2", 0, 4, 1, 1), ("a2", 0, 1, 1, 1),
+    ("a1", 1, 1, 3), ("a2", 0, 2, 0, 1), ("s2", 0, 1, 3), ("b2", 1, 1, 1), ("ca", 2, 0), ("a1", 1, 0, 3),
+    ("b2", 1, 0, 1), ("a2", 1, 1, 0, 1), ("a2", 0, 2, 1, 1), ("a2", 0, 5, 0, 1), ("cb", 2), ("b2", 0, 1, 1),
+    ("a1", 1, 1, 4), ("s2", 1, 0, 3), ("ca", 2, -1), ("a2", 0, 0, 1, 1), ("a2", 0, 4, 0, 1), ("ca", 4, -1),
+    ("ca", 5, 0), ("a2", 0, 1, 0, 1), ("ca", 3, 0), ("a1", 0, 0, 4), ("cb", 1), ("a2", 1, 4, 1, 1),
+    ("a2", 0, 3, 1, 1), ("ca", 6, 0), ("a2", 0, 0, 0, 1), ("a2", 1, 2, 0, 1), ("a2", 0, 5, 1, 1), ("a2", 1, 1, 1, 2),
+    ("b2", 0, 0, 2), ("a2", 1, 5, 0, 1), ("a2", 1, 4, 0, 1), ("s2", 1, 1, 3), ("ca", 0, 1), ("a2", 1, 2, 1, 1),
+    ("ca", 0, -1), ("a2", 1, 5, 1, 1), ("a2", 1, 3, 1, 1), ("ca", 4, 1), ("a2", 1, 0, 1, 2), ("ca", 7, 0),
+    ("s2", 1, 1, 4), ("s2", 0, 0, 4), ("b2", 1, 1, 2), ("ca", 1, 1), ("act", 0), ("a2", 1, 4, 1, 2),
+    ("a2", 0, 5, 0, 2), ("b2", 0, 1, 2), ("a2", 0, 4, 0, 2), ("a2", 1, 6, 0, 1), ("b2", 1, 0, 2), ("cb", 4),
+    ("ca", 4, 2), ("ca", 5, -1), ("a2", 0, 6, 0, 1), ("ca", 3, 1), ("cb", 3), ("a2", 0, 1, 0, 2), ("ca", 5, 1),
+    ("a2", 0, 0, 0, 2), ("a2", 0, 3, 0, 1), ("ca", 1, -1), ("a2", 1, 2, 1, 2), ("ca", 3, -1), ("a2", 0, 2, 0, 2),
+    ("ca", 1, 2), ("ca", 2, 1), ("b2", 0, 0, 3), ("a2", 1, 5, 1, 2), ("b2", 1, 1, 3), ("a2", 0, 6, 1, 1),
+    ("ca", 6, -1), ("ca", 0, 2), ("a2", 1, 6, 1, 1), ("ca", 5, 2), ("ca", 2, 2), ("ca", 6, 1), ("b2", 0, 1, 3),
+    ("cb", 5), ("a2", 1, 7, 1, 1), ("a2", 0, 7, 0, 1), ("b2", 1, 0, 3), ("cb", 6), ("a2", 0, 7, 1, 1), ("ca", 7, -1),
+    ("a2", 1, 7, 0, 1), ("a2", 1, 3, 1, 2), ("ca", 7, 1), ("act", 1), ("a2", 0, 6, 0, 2), ("act", -1),
+    ("a2", 1, 6, 1, 2), ("ca", 6, 2), ("a2", 0, 3, 0, 2), ("ca", 3, 2), ("b2", 1, 1, 4), ("b2", 0, 0, 4), ("cb", 7),
+    ("a2", 0, 7, 0, 2), ("a2", 1, 7, 1, 2), ("ca", 7, 2), ("actb",), ("act", 2),
 )
 
 SCATTER = (
-    ("down", 0), ("down", 1), ("down", 2), ("down", 3), ("down", 4), ("xo", 1), ("yc", 0, 1), ("x2", 1, 0),
-    ("x2", 0, 0), ("xo", 0), ("yc", 1, 1), ("x2", 0, 1), ("x2", 1, 1), ("x2", 1, 3), ("down", 5), ("down", 6),
-    ("xo", 2), ("yo", 1, 2), ("down", 7), ("x2", 1, 2), ("chk",), ("xo", 3), ("yo", 0, 2), ("xo", 5), ("x3", 0),
-    ("zgo",), ("x3", 1), ("x2", 0, 3), ("x2", 0, 4), ("yc", 0, 2), ("yc", 1, 2), ("x2", 0, 2), ("xo", 4),
-    ("yo", 0, 3), ("xo", 6), ("yo", 1, 3), ("chk2",), ("x2", 1, 4), ("yc", 1, 3), ("x2", 0, 5), ("x2", 1, 6),
-    ("yc", 0, 3), ("x2", 1, 5), ("chk3",), ("x2", 0, 6), ("x3", 2), ("zo", 1, 1), ("zc", 0, 1), ("chk4",),
-    ("zc", 1, 1), ("zo", 0, 1), ("yend",), ("x3", 4), ("xo", 7), ("x3", 3), ("zo", 1, 2), ("zc", 0, 2), ("zc", 1, 2),
-    ("zo", 0, 2), ("x3", 6), ("al1",), ("x3", 5), ("b2", 1), ("b2", 0), ("zc", 0, 3), ("x2", 0, 7), ("zo", 1, 3),
-    ("x2", 1, 7), ("al2",), ("zc", 1, 3), ("zo", 0, 3), ("bend",), ("x3", 7), ("aend",),
+    ("down", 0), ("down", 1), ("down", 2), ("x2", 0, 0), ("down", 3), ("xo", 0), ("down", 4), ("down", 5),
+    ("down", 6), ("yc", 1, 1), ("x2", 1, 2), ("x2", 1, 0), ("yc", 0, 1), ("down", 7), ("chk",), ("xo", 2),
+    ("yo", 1, 2), ("xo", 4), ("x2", 0, 2), ("yo", 0, 2), ("x2", 0, 1), ("yc", 0, 2), ("yc", 1, 2), ("x3", 0),
+    ("x2", 1, 3), ("x2", 1, 4), ("x2", 0, 4), ("xo", 3), ("yo", 0, 3), ("x2", 1, 1), ("chk2",), ("zgo",),
+    ("yo", 1, 3), ("x2", 0, 6), ("yc", 1, 3), ("xo", 1), ("x3", 4), ("x3", 2), ("x2", 0, 3), ("x2", 1, 6),
+    ("zo", 1, 1), ("yc", 0, 3), ("xo", 6), ("xo", 5), ("chk3",), ("x3", 1), ("zo", 0, 1), ("chk4",), ("zc", 0, 1),
+    ("zc", 1, 1), ("x2", 1, 5), ("x2", 0, 5), ("yend",), ("x3", 3), ("x2", 0, 7), ("x2", 1, 7), ("x3", 6),
+    ("zo", 0, 2), ("zo", 1, 2), ("zc", 0, 2), ("zc", 1, 2), ("al1",), ("b2", 1), ("b2", 0), ("x3", 5), ("zo", 0, 3),
+    ("zo", 1, 3), ("xo", 7), ("al2",), ("zc", 0, 3), ("zc", 1, 3), ("bend",), ("x3", 7), ("aend",),
 )
 
 
 def kernel(
     n_exp,
     tok_ref, ids_ref, gate_ref, dchk_ref, wg_hbm, wu_hbm, wd_hbm,
-    out_ref, res_ref, alarm_ref,
+    qbuf, aux_ref,
     wg, wu, wd, x, p, acc_ga, acc_ua, acc_gb, acc_ub, hid, fin,
-    sbuf, rbuf, bbuf, qbuf,
+    sbuf, rbuf, bbuf,
     xh, xf, zh, zf, yh, yf, bh, bf,
     racc, cs, cr, cf, zr, cc, es, er, gs, gr,
     w_sem, d_s, d_r, m_s, m_r,
@@ -275,8 +275,6 @@
     for c in w_copies[2 * NT :]:
         c.wait()
 
-    racc[...] = jnp.zeros_like(racc)
-
     def down(tp):
         def one(dp, carry):
             v = jnp.dot(hid[dp], wd[tp], preferred_element_type=F32).astype(BF16)
@@ -286,6 +284,12 @@
             return carry
 
         lax.fori_loop(0, NX, one, 0)
+
+    def down_rows(tp, dp, span):
+        v = jnp.dot(hid[dp, span, :], wd[tp], preferred_element_type=F32).astype(BF16)
+        p[tp, dp, span, :] = v
+        v = v.astype(F32)
+        racc[dp, span, :] = (v[:, 0:128] + v[:, 128:256]) + (v[:, 256:384] + v[:, 384:512]) if cols == 512 else v
 
     def add(tp, dp, span, *others):
         total = p[tp, dp, span, :].astype(F32)
@@ -315,12 +319,19 @@
         if kind == "down":
             (j,) = key
             tp = tz(far[j])
-            down(tp)
+            if j == 0:
+                for n in range(NX):
+                    down_rows(tp, n, B)
+                for i in range(2):
+                    post(p.at[tp, :, side_b[i][0]], yh.at[i], i, zdev[i], "yc", 0)
+                down_rows(tp, dx(2), A)
+            else:
+                down(tp)
             for i in range(2):
                 post(p.at[tp, dx(2), side_a[i][0]], xh.at[j, i], i, xdev[i], "xh", j)
             if j == 0:
-                for i in range(2):
-                    post(p.at[tp, :, side_b[i][0]], yh.at[i], i, zdev[i], "yc", 0)
+                for n in (1, -1, 0):
+                    down_rows(tp, dx(n), A)
             if j in (1, 2):
                 i = j - 1
                 post(p.at[tp, :, side_b[i][1]], yf.at[0, i, :, slot_b[i][1]], i, zdev[i], "yo", 1)
@@ -421,7 +432,6 @@
             send(cf.at[1], cc.at[j], cc_s.at[j - 1], cc_r.at[j - 1], (source(j), t, d))
 
     iota_s = lax.broadcasted_iota(jnp.int32, (toks, rows), 1).astype(F32)
-    route = {}
 
     def chk4():
         iota_l = lax.broadcasted_iota(jnp.int32, (toks, toks), 1).astype(F32)
@@ -448,14 +458,17 @@
             picked = jnp.where(iota_s == place, row, 0.0)
             diff = diff + weight[k] * jnp.sum(picked, axis=1, keepdims=True)
         residual = jnp.transpose(jnp.broadcast_to(diff, (toks, toks)))[0:1] * (1.0 / math.sqrt(D))
-        res_ref[...] = residual
+        aux_ref[toks : toks + 1, :] = residual
         score = jnp.broadcast_to(jnp.sum(residual * residual, axis=1, keepdims=True), (1, toks))
         es[...] = score
         for o in range(1, NX):
             send(es, er.at[d], es_s.at[o - 1], es_r.at[o - 1], (e, t, dx(o)))
         er[d] = score
-        route["weight"] = weight
-        route["slot"] = [col[k] * float(CAP) + pos[k] for k in range(2)]
+        table = jnp.zeros((toks, toks), F32)
+        for k in range(2):
+            table = jnp.where(iota_l == float(k), col[k] * float(CAP) + pos[k], table)
+            table = jnp.where(iota_l == float(2 + k), weight[k], table)
+        aux_ref[0:toks, :] = table
 
     def al1():
         for o in range(1, NX):
@@ -474,7 +487,7 @@
         score = gr[0]
         for i in range(1, n_exp):
             score = score + gr[i]
-        alarm_ref[...] = score[0:1, 0:1] * (1.0 / (toks * n_exp * NX))
+        aux_ref[toks + 1 : toks + 2, :] = score * (1.0 / (toks * n_exp * NX))
 
     CHECKS = {"chk": chk, "chk2": chk2, "chk3": chk3, "chk4": chk4, "al1": al1, "al2": al2}
     for step in SCATTER:
@@ -482,12 +495,6 @@
 
     for j in range(1, n_exp):
         got(qbuf.at[expert_at(j)], q_s.at[j - 1], q_r.at[j - 1])
-    back = qbuf[...].astype(F32).reshape(rows, cols).astype(BF16)
-    combined = jnp.zeros((toks, cols), F32)
-    for k in range(2):
-        sel = (iota_s == route["slot"][k]).astype(F32).astype(BF16)
-        combined = combined + route["weight"][k] * jnp.dot(sel, back, preferred_element_type=F32)
-    out_ref[...] = combined
 
     for o in range(n_exp - 1):
         sent(sbuf.at[0], d_s.at[o], d_r.at[o])
@@ -501,6 +508,21 @@
         sent(cf.at[0], z_s.at[o], z_r.at[o])
     for ref, n in used:
         sent(ref, m_s.at[n], m_r.at[n])
+
+
+def combine(back_ref, aux_ref, out_ref, res_ref, alarm_ref):
+    n_exp, cap, cols = back_ref.shape
+    toks = out_ref.shape[0]
+    rows = n_exp * cap
+    back = back_ref[...].astype(F32).reshape(rows, cols).astype(BF16)
+    iota_s = lax.broadcasted_iota(jnp.int32, (toks, rows), 1).astype(F32)
+    total = jnp.zeros((toks, cols), F32)
+    for k in range(2):
+        sel = (iota_s == aux_ref[0:toks, k : k + 1]).astype(F32).astype(BF16)
+        total = total + aux_ref[0:toks, 2 + k : 3 + k] * jnp.dot(sel, back, preferred_element_type=F32)
+    out_ref[...] = total
+    res_ref[...] = aux_ref[toks : toks + 1, :]
+    alarm_ref[...] = aux_ref[toks + 1 : toks + 2, 0:1]
 
 
 def body(tokens, expert_ids, gate_fixed, w_gate, w_up, w_down, down_check):
@@ -518,8 +540,7 @@
         vm((NT, NX, rows, cols), BF16), vm((NT, NX, rows, cols), BF16),
         vm((NX, na, ff), F32), vm((NX, na, ff), F32), vm((NX * nb, ff), F32), vm((NX * nb, ff), F32),
         vm((NX, rows, ff), BF16), vm((rows, cols), F32),
-        vm((n_exp, CAP, cols), BF16), vm((n_exp, CAP, cols), BF16),
-        vm((n_exp, CAP, cols), BF16), vm((n_exp, CAP, cols), BF16),
+        vm((n_exp, CAP, cols), BF16), vm((n_exp, CAP, cols), BF16), vm((n_exp, CAP, cols), BF16),
         vm((NT, 2, na // 2, cols), BF16), vm((NT, 2, na, cols), BF16),
         vm((2, na // 2, cols), BF16), vm((3, 2, na, cols), BF16),
         vm((2, NX, nb // 2, cols), BF16), vm((3, 2, NX, nb, cols), BF16),
@@ -533,15 +554,14 @@
     ]
     vmem = pl.BlockSpec(memory_space=pltpu.VMEM)
     hbm = pl.BlockSpec(memory_space=pl.ANY)
-    mix, residual, alarm = pl.pallas_call(
+    back, aux = pl.pallas_call(
         functools.partial(kernel, n_exp),
         out_shape=(
-            jax.ShapeDtypeStruct((toks, cols), F32),
-            jax.ShapeDtypeStruct((1, toks), F32),
-            jax.ShapeDtypeStruct((1, 1), F32),
+            jax.ShapeDtypeStruct((n_exp, CAP, cols), BF16),
+            jax.ShapeDtypeStruct((toks + 8, toks), F32),
         ),
         in_specs=[vmem, vmem, vmem, vmem, hbm, hbm, hbm],
-        out_specs=(vmem, vmem, vmem),
+        out_specs=(vmem, vmem),
         scratch_shapes=scratch,
         compiler_params=pltpu.CompilerParams(
             collective_id=0, has_side_effects=True, vmem_limit_bytes=66_000_000
@@ -550,6 +570,16 @@
         tokens, expert_ids.T, gate_fixed.T, down_check,
         w_gate[0].T, w_up[0].T, w_down[0],
     )
+    mix, residual, alarm = pl.pallas_call(
+        combine,
+        out_shape=(
+            jax.ShapeDtypeStruct((toks, cols), F32),
+            jax.ShapeDtypeStruct((1, toks), F32),
+            jax.ShapeDtypeStruct((1, 1), F32),
+        ),
+        in_specs=[vmem, vmem],
+        out_specs=(vmem, vmem, vmem),
+    )(back, aux)
     return mix, residual.reshape(toks), alarm.reshape(())
 
 

time: 149 us -> 144 us (0.966)
  local copies, waits for them, and re-layouts: 2.8 us -> 0 us
  between operations: 2.32 us -> 0.64 us
    pallas_call x1, Pallas kernels: 144 us -> 141 us  [body(): pl.pallas_call(functools.partial(kernel, n_exp), out_shape=(jax.ShapeDtyp...]
    unnamed x2 -> x0, local copies, waits for them, and re-layouts: 2.8 us -> none
    pallas_call x0 -> x1, Pallas kernels: none -> 2.03 us  [body(): pl.pallas_call(combine, out_shape=(jax.ShapeDtypeStruct((toks, cols), F32...]
where the time goes in v4:
time: 144 us
  Pallas kernels  143 us (99%)
    pallas_call x1, Pallas kernels, body(): pl.pallas_call(functools.partial(kernel, n_exp), out_shape=(jax.ShapeDtyp...  141 us

profile of v4, /device:TPU:1, one launch (start us, length us, event | category | flops | bytes accessed | tf_op | source)
XLA Modules:
  0.0 143.5 jit_solution(12959706944163520429)
XLA Ops:
  0.6 140.8 %shard_map.94 = (bf16[8,40,512]{2,1,0:T(8,128)(2,1)}, f32[136,128]{1,0:T(8,128)}) custom-call(bf16[128,512]{1,0:T(8,128)(2,1)} %tok_ref.1, s32[2,128]{1,0:T(2,128)} %bitcast.14, s32[2,128]{1,0:T(2,128)} %bitcast.15, bf16[1,448]{1,0:T(2,128)(2,1)} %dchk_ref.1, bf16[448,4096]{1,0:T(8,128)(2,1)} %bitcast.11, bf16[448,4096]{1,0:T(8,128)(2,1)} %bitcast.12, ...), custom_call_target="tpu_custom_call" | custom-call | tf_op jit(solution)/shard_map/pallas_call | solution.py:557
  141.5 2.0 %shard_map.95 = (f32[128,512]{1,0:T(8,128)}, f32[1,128]{1,0:T(1,128)}, f32[1,1]{1,0:T(1,128)}) custom-call(bf16[8,40,512]{2,1,0:T(8,128)(2,1)} %get-tuple-element.8.back_ref, f32[136,128]{1,0:T(8,128)} %get-tuple-element.9.aux_ref), custom_call_target="tpu_custom_call" | custom-call | tf_op jit(solution)/shard_map/pallas_call | solution.py:573
